TPU v7x, 256 devices: a whole 4x4x8 slice. The times are simulated.
256 devices in a mesh: front: 4 (over y_lo, core), blk: 64 (over y_hi, x, z).
Axes of the slice: x: 4, y: 4 (y_hi: 2, y_lo: 2; y = y_hi * 2 + y_lo), z: 8, core: 2. Of those that a mesh axis runs over, the one named last changes fastest.
Arguments:
- front: float32 [4, 8192, 8192], P('front', 'blk'), parts along dimension 0, may hold values from -8 to 40, as said below
- child: float32 [4, 4096, 4096], P('front', 'blk'), parts along dimension 0, may hold values from -1 to 4, as said below
- index_map: int32 [16384], P('front'), parts along dimension 0, may hold values from 0 to 8191, as said below
Outputs:
- factored: float32 [4, 8192, 8192], P('front', 'blk'), parts along dimension 0
There are 4 independent parts, one for each index of `front`. A program takes and returns all parts, laid end to end along the dimension named above; each array names one. Nothing has to cross between parts.
Inputs may be any that keep to these rules, and one draw needn't show every extreme that they name: front is symmetric and positive definite. child is symmetric and positive semidefinite. `index_map`: tile t of the child (indices t * 64 to t * 64 + 63, with t = k * 64 + e and e < 64) maps in increasing order onto 64 different indices of the front's block column b = k * 64 + ((e + h) mod 64), where h is half of 64, that is onto indices b * 128 to b * 128 + 127; no two child indices share a front index.
All inputs are finite; a program needn't handle non-finite values.
Results may differ from a plain program's by a relative error of at most 0.0034.
Values may be sent and summed in bfloat16 or wider, within the bound.
A program may use at most 128 MiB of HBM per device.

v0:
```python
import jax
import jax.numpy as jnp
from jax import lax
from jax.sharding import PartitionSpec as P

PANEL_WIDTH = 512
BLOCK_WIDTH = 128
COL_BLOCKS = 1
TILE_WIDTH = 64


HIGHEST = lax.Precision.HIGHEST


def split_up(shard, dim, count):
    before, after = (shard.shape[:dim], shard.shape[dim + 1 :])
    return jnp.moveaxis(shard.reshape(*before, count, -1, *after), dim, 0)


def sent_and_summed(shard, axis, dim):
    count = lax.axis_size(axis)
    pieces = lax.all_to_all(split_up(shard, dim, count), axis, 0, 0, tiled=True)
    return jnp.sum(pieces, axis=0)


def filled_up(lines, count):
    spare = -lines.shape[0] % count
    if not spare:
        return lines
    return jnp.concatenate([lines, jnp.zeros((spare, *lines.shape[1:]), lines.dtype)])


def from_everyone(shard, axis):
    copies = jnp.broadcast_to(shard, (lax.axis_size(axis), *shard.shape))
    return lax.all_to_all(copies, axis, split_axis=0, concat_axis=0, tiled=True)


def in_order(pieces, dim):
    shape = list(pieces.shape[1:])
    shape[dim] *= pieces.shape[0]
    return jnp.moveaxis(pieces, 0, dim).reshape(shape)


def gathered_copies(shard, axis, dim):
    pieces = from_everyone(shard, axis)
    return in_order(pieces, dim)


def total_of(shard, axes):
    lines = shard.reshape(-1, shard.shape[-1])
    own = sent_and_summed(filled_up(lines, lax.axis_size(axes)), axes, 0)
    whole = gathered_copies(own, axes, 0)
    return whole[: len(lines)].reshape(shard.shape)


def from_behind(shard, axis, by):
    count = lax.axis_size(axis)
    return lax.ppermute(shard, axis, [(i, (i + by) % count) for i in range(count)])


def column_numbers(cycle_size, my_index):
    local_ids = jnp.arange(COL_BLOCKS * BLOCK_WIDTH, dtype=jnp.int32)
    return (
        local_ids // BLOCK_WIDTH * cycle_size + my_index
    ) * BLOCK_WIDTH + local_ids % BLOCK_WIDTH


def row_numbers(cycle_size):
    stored = jnp.arange(cycle_size * COL_BLOCKS * BLOCK_WIDTH, dtype=jnp.int32)
    holder = stored // (COL_BLOCKS * BLOCK_WIDTH)
    within = stored // BLOCK_WIDTH % COL_BLOCKS
    return (within * cycle_size + holder) * BLOCK_WIDTH + stored % BLOCK_WIDTH


def cycle_rows(matrix, cycle_size):
    height = matrix.shape[0]
    return (
        matrix.reshape(height, COL_BLOCKS, cycle_size, BLOCK_WIDTH)
        .transpose(0, 2, 1, 3)
        .reshape(height, -1)
    )


def natural_rows(matrix, cycle_size):
    height = matrix.shape[0]
    return (
        matrix.reshape(height, cycle_size, COL_BLOCKS, BLOCK_WIDTH)
        .transpose(0, 2, 1, 3)
        .reshape(height, -1)
    )


def panel_rows(matrix, row_start, cycle_size):
    first_owner = row_start // BLOCK_WIDTH
    owner_count = PANEL_WIDTH // BLOCK_WIDTH
    height = matrix.shape[0]
    blocks = matrix.reshape(height, cycle_size, COL_BLOCKS, BLOCK_WIDTH)
    return blocks[:, first_owner : first_owner + owner_count, 0, :].reshape(height, PANEL_WIDTH)


def ownership(row_start, my_index):
    first_owner = row_start // BLOCK_WIDTH
    owner_count = PANEL_WIDTH // BLOCK_WIDTH
    is_owner = (my_index >= first_owner) & (my_index < first_owner + owner_count)
    column_start = jnp.clip(my_index - first_owner, 0, owner_count - 1) * BLOCK_WIDTH
    return (is_owner, column_start)


def collect(stacked, row_start, my_index):
    is_owner, column_start = ownership(row_start, my_index)
    padded = jnp.zeros((stacked.shape[0], PANEL_WIDTH, PANEL_WIDTH), jnp.float32)
    padded = lax.dynamic_update_slice(
        padded, jnp.where(is_owner, stacked, 0.0), (0, column_start, 0)
    )
    result = total_of(padded, "blk")
    return result


def own_rows(diag_factor, panel_part, row_start, columns):
    solved = lax.linalg.triangular_solve(
        diag_factor, panel_part, left_side=False, lower=True, transpose_a=True
    )
    offsets = columns - row_start
    diag_rows = jnp.take(diag_factor, jnp.clip(offsets, 0, PANEL_WIDTH - 1), axis=0)
    inside = (offsets >= 0) & (offsets < PANEL_WIDTH)
    before = offsets < 0
    return jnp.where(inside[:, None], diag_rows, jnp.where(before[:, None], 0.0, solved))


def make_refresh(working, lowered, owned_panels, received):
    updated = working - lax.dot_general(
        lowered, received, (((1,), (1,)), ((), ())), preferred_element_type=jnp.float32
    )
    leading = updated
    for is_owner, column_start in owned_panels:
        factor_column = (
            lax.dynamic_slice_in_dim(received, column_start, BLOCK_WIDTH, 1).astype(jnp.float32).T
        )
        leading = jnp.where(is_owner, factor_column, leading)
    return jnp.concatenate([leading, updated[BLOCK_WIDTH:]], axis=0)


def assemble(front, child, index_map, cycle_size, my_index):
    half_cycle = cycle_size // 2
    arrived_tiles = from_behind(child, "blk", half_cycle)
    full_order = 2 * index_map.shape[0]
    tile_places = (index_map % BLOCK_WIDTH).reshape(COL_BLOCKS, cycle_size, TILE_WIDTH)
    places = jnp.arange(BLOCK_WIDTH, dtype=jnp.int32)
    row_table = (tile_places[..., None] == places).astype(jnp.float32)
    shaped = arrived_tiles.reshape(COL_BLOCKS, TILE_WIDTH, COL_BLOCKS, cycle_size, TILE_WIDTH)
    spread = jnp.einsum("acbei,beiq->acbeq", shaped, row_table, precision=HIGHEST)
    spread = jnp.roll(spread, half_cycle, axis=3).reshape(COL_BLOCKS, TILE_WIDTH, full_order)
    source = (my_index - half_cycle) % cycle_size
    own_places = lax.dynamic_index_in_dim(tile_places, source, axis=1, keepdims=False)
    column_table = (own_places[..., None] == places).astype(jnp.float32)
    placed = jnp.einsum("kcq,kcn->kqn", column_table, spread, precision=HIGHEST)
    return front + placed


def on_device(front, child, index_map):
    cycle_size = lax.axis_size("blk")
    my_index = lax.axis_index("blk")
    local_width = COL_BLOCKS * BLOCK_WIDTH
    assembled = assemble(front, child, index_map, cycle_size, my_index).reshape(local_width, -1)
    working = cycle_rows(assembled, cycle_size)
    columns = column_numbers(cycle_size, my_index)
    first_part = panel_rows(working, 0, cycle_size)
    first_diag = collect(first_part[None, :BLOCK_WIDTH], 0, my_index)[0]
    first_rows = own_rows(jnp.linalg.cholesky(first_diag), first_part, 0, columns).astype(
        jnp.bfloat16
    )
    second_part = panel_rows(working, PANEL_WIDTH, cycle_size)
    shared = collect(
        jnp.stack([second_part, first_rows.astype(jnp.float32)]), PANEL_WIDTH, my_index
    )
    crossing = shared[1].astype(jnp.bfloat16)
    second_diag = shared[0] - jnp.dot(crossing, crossing.T, preferred_element_type=jnp.float32)
    second_part = second_part - lax.dot_general(
        first_rows, crossing, (((1,), (1,)), ((), ())), preferred_element_type=jnp.float32
    )
    second_rows = own_rows(
        jnp.linalg.cholesky(second_diag), second_part, PANEL_WIDTH, columns
    ).astype(jnp.bfloat16)
    lowered = jnp.concatenate([first_rows, second_rows], axis=1)
    first_owner = ownership(0, my_index)
    second_owner = ownership(PANEL_WIDTH, my_index)
    owned_panels = (first_owner, (second_owner[0], second_owner[1] + PANEL_WIDTH))
    working = make_refresh(
        working, lowered, owned_panels, lax.all_gather(lowered, "blk", axis=0, tiled=True)
    )
    trailing = columns >= 2 * PANEL_WIDTH
    leading_rows = row_numbers(cycle_size) < 2 * PANEL_WIDTH
    working = jnp.where(trailing[:, None] & leading_rows[None, :], 0.0, working)
    return natural_rows(working, cycle_size).reshape(COL_BLOCKS, BLOCK_WIDTH, -1)


def solution(mesh):
    placed = (P("front", "blk", None), P("front", "blk", None), P("front"))
    return jax.shard_map(
        on_device, mesh=mesh, in_specs=placed, out_specs=P("front", "blk", None), check_vma=False
    )
```

profile of v0, /device:TPU:8, one launch (start us, length us, event | category | flops | bytes accessed | tf_op | source)
XLA Modules:
  0.0 722.1 jit_solution(17179738872541720833)
XLA Ops:
  6.5 2.3 collective-permute-start
  9.7 23.4 %collective-permute-done = f32[1,64,4096]{2,1,0:T(8,128)S(1)} collective-permute-done((f32[1,64,4096]{2,1,0:T(8,128)}, f32[1,64,4096]{2,1,0:T(8,128)S(1)}, u32[]{:S(2)}, u32[]{:S(2)}) %collective-permute-start) | collective-permute-done | bytes 1048608 | tf_op jit(solution)/shard_map/ppermute | solution.py:58
  34.0 3.4 fusion.9
  37.9 1.2 copy.12
  40.1 3.3 fusion
  44.1 1.3 copy-done
  45.8 42.7 %all_to_all.20 = f32[64,8,512]{2,1,0:T(8,128)S(1)} all-to-all(f32[64,8,512]{2,1,0:T(8,128)S(1)} %bitcast.161), channel_id=1, replica_groups=mesh['front'=4,'blk'=64] {'blk'}, dimensions={0} | all-to-all | bytes 2097152 | tf_op jit(solution)/shard_map/all_to_all | solution.py:22
  88.6 1.1 broadcast_in_dim.78
  89.7 6.5 all-to-all-start.1
  98.8 25.9 %all-to-all-done.1 = f32[64,8,512]{2,1,0:T(8,128)S(1)} async-done(((f32[64,8,512]{2,1,0:T(8,128)}), f32[64,8,512]{2,1,0:T(8,128)S(1)}, u32[]{:S(2)}, u32[]{:S(2)}) %all-to-all-start.1) | async-done | bytes 1048608 | tf_op jit(solution)/shard_map/all_to_all | solution.py:35
  125.3 11.7 %cholesky.286 = f32[128,128]{1,0:T(8,128)S(1)} custom-call(f32[128,128]{1,0:T(8,128)S(1)} %cholesky.426), custom_call_target="Cholesky" | custom-call | tf_op jit(solution)/shard_map/jit(cholesky)/cholesky | solution.py:169
  137.2 9.8 %custom-call.27 = f32[1,128,128]{1,2,0:T(8,128)S(1)} custom-call(f32[1,128,128]{2,1,0:T(8,128)S(1)} %get-tuple-element.74), custom_call_target="InvertDiagBlocksLowerTriangular" | custom-call | tf_op jit(solution)/shard_map/jit(cholesky)/cholesky | solution.py:169
  147.6 11.7 %cholesky.305 = f32[128,128]{1,0:T(8,128)S(1)} custom-call(f32[128,128]{1,0:T(8,128)S(1)} %cholesky.430), custom_call_target="Cholesky" | custom-call | tf_op jit(solution)/shard_map/jit(cholesky)/cholesky | solution.py:169
  159.4 10.0 %custom-call.28 = f32[1,128,128]{1,2,0:T(8,128)S(1)} custom-call(f32[1,128,128]{2,1,0:T(8,128)S(1)} %get-tuple-element.71), custom_call_target="InvertDiagBlocksLowerTriangular" | custom-call | tf_op jit(solution)/shard_map/jit(cholesky)/cholesky | solution.py:169
  170.1 11.7 %cholesky.326 = f32[128,128]{1,0:T(8,128)S(1)} custom-call(f32[128,128]{1,0:T(8,128)S(1)} %cholesky.435), custom_call_target="Cholesky" | custom-call | tf_op jit(solution)/shard_map/jit(cholesky)/cholesky | solution.py:169
  182.5 9.8 %custom-call.29 = f32[1,128,128]{1,2,0:T(8,128)S(1)} custom-call(f32[1,128,128]{2,1,0:T(8,128)S(1)} %get-tuple-element.68), custom_call_target="InvertDiagBlocksLowerTriangular" | custom-call | tf_op jit(solution)/shard_map/jit(cholesky)/cholesky | solution.py:169
  192.9 11.7 %cholesky.343 = f32[128,128]{1,0:T(8,128)S(1)} custom-call(f32[128,128]{1,0:T(8,128)S(1)} %convolution_subtract_fusion.14), custom_call_target="Cholesky" | custom-call | tf_op jit(solution)/shard_map/jit(cholesky)/cholesky | solution.py:169
  209.1 8.0 %while.4 = (s32[]{:T(128)}, f32[512,512]{1,0:T(8,128)S(1)}, s32[4,2]{0,1:T(2,128)S(1)}, f32[4,128,128]{2,1,0:T(8,128)S(1)}, s32[]{:T(128)}) while((s32[]{:T(128)}, f32[512,512]{1,0:T(8,128)S(1)}, s32[4,2]{0,1:T(2,128)S(1)}, f32[4,128,128]{2,1,0:T(8,128)S(1)}, s32[]{:T(128)}) %tuple.64), condition=%wide.while_cond, body=%wide.while_body.sunk | while | flops 2 | bytes 131181 | solution.py:120
  209.8 1.3 bitcast_dynamic-update-slice_fusion.4
  211.8 1.3 bitcast_dynamic-update-slice_fusion.4
  213.8 1.3 bitcast_dynamic-update-slice_fusion.4
  215.8 1.3 bitcast_dynamic-update-slice_fusion.4
  217.2 39.3 %custom-call.30 = f32[4,128,128]{1,2,0:T(8,128)S(1)} custom-call(f32[4,128,128]{2,1,0:T(8,128)S(1)} %get-tuple-element.22), custom_call_target="InvertDiagBlocksLowerTriangular" | custom-call | tf_op jit(solution)/shard_map/triangular_solve/custom-call.3 | solution.py:120
  260.5 55.7 %all_to_all.21 = f32[64,16,512]{2,1,0:T(8,128)S(1)} all-to-all(f32[64,16,512]{2,1,0:T(8,128)S(1)} %bitcast.158), channel_id=1, replica_groups=mesh['front'=4,'blk'=64] {'blk'}, dimensions={0} | all-to-all | bytes 4194304 | tf_op jit(solution)/shard_map/all_to_all | solution.py:22
  316.3 1.6 broadcast_in_dim.84
  317.9 7.6 %all-to-all-start.3 = ((f32[64,16,512]{2,1,0:T(8,128)}), f32[64,16,512]{2,1,0:T(8,128)S(1)}, u32[]{:S(2)}, u32[]{:S(2)}) async-start(f32[64,16,512]{2,1,0:T(8,128)} %broadcast_in_dim.84), calls=%async_computation.3 | async-start | bytes 4194304 | tf_op jit(solution)/shard_map/all_to_all | solution.py:35
  326.6 47.4 %all-to-all-done.3 = f32[64,16,512]{2,1,0:T(8,128)S(1)} async-done(((f32[64,16,512]{2,1,0:T(8,128)}), f32[64,16,512]{2,1,0:T(8,128)S(1)}, u32[]{:S(2)}, u32[]{:S(2)}) %all-to-all-start.3) | async-done | bytes 2097184 | tf_op jit(solution)/shard_map/all_to_all | solution.py:35
  375.1 2.6 copy.17
  377.8 1.7 convolution_subtract_fusion.1
  381.1 11.7 %cholesky.358 = f32[128,128]{1,0:T(8,128)S(1)} custom-call(f32[128,128]{1,0:T(8,128)S(1)} %cholesky.439), custom_call_target="Cholesky" | custom-call | tf_op jit(solution)/shard_map/jit(cholesky)/cholesky | solution.py:182
  392.9 9.8 %custom-call.31 = f32[1,128,128]{1,2,0:T(8,128)S(1)} custom-call(f32[1,128,128]{2,1,0:T(8,128)S(1)} %get-tuple-element.64), custom_call_target="InvertDiagBlocksLowerTriangular" | custom-call | tf_op jit(solution)/shard_map/jit(cholesky)/cholesky | solution.py:182
  402.8 1.2 constant_dynamic-update-slice_fusion.3
  404.0 1.3 convolution_subtract_fusion.3
  405.3 11.7 %cholesky.377 = f32[128,128]{1,0:T(8,128)S(1)} custom-call(f32[128,128]{1,0:T(8,128)S(1)} %cholesky.443), custom_call_target="Cholesky" | custom-call | tf_op jit(solution)/shard_map/jit(cholesky)/cholesky | solution.py:182
  418.4 9.9 %custom-call.32 = f32[1,128,128]{1,2,0:T(8,128)S(1)} custom-call(f32[1,128,128]{2,1,0:T(8,128)S(1)} %get-tuple-element.61), custom_call_target="InvertDiagBlocksLowerTriangular" | custom-call | tf_op jit(solution)/shard_map/jit(cholesky)/cholesky | solution.py:182
  428.6 1.3 convolution_subtract_fusion.5
  429.9 11.7 %cholesky.398 = f32[128,128]{1,0:T(8,128)S(1)} custom-call(f32[128,128]{1,0:T(8,128)S(1)} %cholesky.448), custom_call_target="Cholesky" | custom-call | tf_op jit(solution)/shard_map/jit(cholesky)/cholesky | solution.py:182
  442.3 9.8 %custom-call.33 = f32[1,128,128]{1,2,0:T(8,128)S(1)} custom-call(f32[1,128,128]{2,1,0:T(8,128)S(1)} %get-tuple-element.58), custom_call_target="InvertDiagBlocksLowerTriangular" | custom-call | tf_op jit(solution)/shard_map/jit(cholesky)/cholesky | solution.py:182
  452.3 1.3 convolution_subtract_fusion.12
  453.6 11.9 %cholesky.415 = f32[128,128]{1,0:T(8,128)S(1)} custom-call(f32[128,128]{1,0:T(8,128)S(1)} %convolution_subtract_fusion.12), custom_call_target="Cholesky" | custom-call | tf_op jit(solution)/shard_map/jit(cholesky)/cholesky | solution.py:182
  469.0 8.1 %while.5 = (s32[]{:T(128)}, f32[512,512]{1,0:T(8,128)S(1)}, s32[4,2]{0,1:T(2,128)S(1)}, f32[4,128,128]{2,1,0:T(8,128)S(1)}, s32[]{:T(128)}) while((s32[]{:T(128)}, f32[512,512]{1,0:T(8,128)S(1)}, s32[4,2]{0,1:T(2,128)S(1)}, f32[4,128,128]{2,1,0:T(8,128)S(1)}, s32[]{:T(128)}) %tuple.72), condition=%wide.while_cond.clone, body=%wide.while_body.clone.sunk | while | flops 2 | bytes 131181 | solution.py:120
  469.7 1.3 bitcast_dynamic-update-slice_fusion.5
  471.7 1.3 bitcast_dynamic-update-slice_fusion.5
  473.8 1.3 bitcast_dynamic-update-slice_fusion.5
  475.8 1.3 bitcast_dynamic-update-slice_fusion.5
  477.2 39.3 %custom-call.34 = f32[4,128,128]{1,2,0:T(8,128)S(1)} custom-call(f32[4,128,128]{2,1,0:T(8,128)S(1)} %get-tuple-element.23), custom_call_target="InvertDiagBlocksLowerTriangular" | custom-call | tf_op jit(solution)/shard_map/triangular_solve/custom-call.3 | solution.py:120
  521.0 180.0 %all-gather.2.cloned.1.call-done = bf16[8192,1024]{0,1:T(8,128)(2,1)} async-done(((bf16[128,1024]{0,1:T(8,128)(2,1)}), bf16[8192,1024]{0,1:T(8,128)(2,1)}) %all-gather.2.cloned.1.call-update) | async-done | bytes 16777232 | tf_op jit(solution)/shard_map/all_gather | solution.py:189
  701.0 13.8 %fusion.4 = f32[1,128,8192]{2,1,0:T(8,128)} fusion(bf16[8192,1024]{0,1:T(8,128)(2,1)} %all-gather.2.cloned.1.call-done, f32[1,128,8192]{2,1,0:T(8,128)} %copy-done, s32[]{:T(128)S(6)} %select_n.184, s32[]{:T(128)S(6)} %select_n.182, pred[]{:T(512)S(6)} %and.158, pred[]{:T(512)S(6)} %and.156, pred[8192]{0:T(1024)(128)(4,1)S(1)} %fusion.83, ...), kind=kOutput, calls=%fused_computation.12 | convolution fusion | flops 2155347968 | bytes 29630602 | tf_op jit(solution)/shard_map/dot_general | solution.py:131
  (129 shorter events, 33.3 us)
Async XLA Ops:
  6.5 26.6 %collective-permute-start = (f32[1,64,4096]{2,1,0:T(8,128)}, f32[1,64,4096]{2,1,0:T(8,128)S(1)}, u32[]{:S(2)}, u32[]{:S(2)}) collective-permute-start(f32[1,64,4096]{2,1,0:T(8,128)} %param.9), channel_id=1, source_target_pairs={{0,32},{1,33},{2,34},{3,35},{4,36},{5,37},{6,38},{7,39},{8,40},{9,... | collective-permute-start | bytes 3145736 | tf_op jit(solution)/shard_map/ppermute | solution.py:58
  37.9 2.2 copy-start.1
  43.4 2.0 copy-start
  89.7 35.0 %all-to-all-start.1 = ((f32[64,8,512]{2,1,0:T(8,128)}), f32[64,8,512]{2,1,0:T(8,128)S(1)}, u32[]{:S(2)}, u32[]{:S(2)}) async-start(f32[64,8,512]{2,1,0:T(8,128)} %broadcast_in_dim.78), calls=%async_computation.1 | async-start | bytes 2097152 | tf_op jit(solution)/shard_map/all_to_all | solution.py:35
  192.9 63.6 %copy-start.3 = (f32[16,8,4,128]{3,1,2,0:T(8,128)S(1)}, f32[16,8,4,128]{3,1,2,0:T(8,128)}, u32[]{:S(2)}) copy-start(f32[16,8,4,128]{3,1,2,0:T(8,128)} %copy.37) | copy-start | bytes 786436
  209.1 50.7 %copy-start.6 = (pred[128]{0:T(512)(128)(4,1)S(1)}, pred[128]{0:T(512)(128)(4,1)}, u32[]{:S(2)}) copy-start(pred[128]{0:T(512)(128)(4,1)} %get-tuple-element.84) | copy-start | bytes 388
  209.1 50.7 %copy-start.7 = (pred[128]{0:T(512)(128)(4,1)S(1)}, pred[128]{0:T(512)(128)(4,1)}, u32[]{:S(2)}) copy-start(pred[128]{0:T(512)(128)(4,1)} %get-tuple-element.86) | copy-start | bytes 388
  317.9 7.8 %copy-start.8 = (s32[128]{0:T(128)S(1)}, s32[128]{0:T(128)}, u32[]{:S(2)}) copy-start(s32[128]{0:T(128)} %get-tuple-element.79) | copy-start | bytes 1540
  317.9 56.1 %all-to-all-start.3 = ((f32[64,16,512]{2,1,0:T(8,128)}), f32[64,16,512]{2,1,0:T(8,128)S(1)}, u32[]{:S(2)}, u32[]{:S(2)}) async-start(f32[64,16,512]{2,1,0:T(8,128)} %broadcast_in_dim.84), calls=%async_computation.3 | async-start | bytes 4194304 | tf_op jit(solution)/shard_map/all_to_all | solution.py:35
  325.5 375.5 %all-gather.2.cloned.1.call-start = ((), (), s32[]{:S(2)}) async-start(), calls=%async_computation.4 | async-start | bytes 17039360 | tf_op jit(solution)/shard_map/all_gather | solution.py:189
  380.1 1.0 copy-start.2
  452.3 64.2 %copy-start.4 = (f32[128,512]{1,0:T(8,128)S(1)}, f32[128,512]{1,0:T(8,128)}, u32[]{:S(2)}) copy-start(f32[128,512]{1,0:T(8,128)} %copy.23) | copy-start | bytes 786436
  516.5 3.7 copy-start.5
Sparse Core Ops, SparseCore 0:
  521.1 179.9 all-gather.1
where the time goes:
time: 730 us; the launch traced here: 722 us
  waiting for transfers between devices  277 us (38%)
  other arithmetic  242 us (33%)
  blocking collectives  98.4 us (13%)
  matrix products  34.4 us (5%)
  local copies, waits for them, and re-layouts  34.3 us (5%)
  between operations  19.6 us (3%)
  starting transfers between devices  16.6 us (2%)
    all_gather x1, waiting for transfers between devices, on_device(): lax.all_gather(lowered, 'blk', axis=0, tiled=True)  180 us
    all_to_all x2, blocking collectives, sent_and_summed(): pieces = lax.all_to_all(split_up(shard, dim, count), axis, 0, 0, tiled=True)  98.4 us
    another operation x15, other arithmetic, on_device(): jnp.linalg.cholesky(second_diag)  79.5 us
    another operation x14, other arithmetic, on_device(): jnp.linalg.cholesky(first_diag)  79 us
    another operation x5, other arithmetic, own_rows(): lax.linalg.triangular_solve(diag_factor, panel_part, left_side=False, low...  79 us
    all_to_all x2, waiting for transfers between devices, from_everyone(): return lax.all_to_all(copies, axis, split_axis=0, concat_axis=0, tiled=True)  73.3 us
    ppermute x1, waiting for transfers between devices, from_behind(): lax.ppermute(shard, axis, [(i, (i + by) % count) for i in range(count)])  23.4 us
    another operation x27, local copies, waits for them, and re-layouts, own_rows(): lax.linalg.triangular_solve(diag_factor, panel_part, left_side=False, low...  16 us
  transfers between devices with their start and end apart: 4, of which 4 were waited for; matrix products, arithmetic and copies ran while one was open for 1% of the time, Pallas kernels for 0%

commit v1 on v0

v1 whole, which is shorter than its diff:
```python
import jax
import jax.numpy as jnp
from jax import lax
from jax.experimental import pallas as pl
from jax.experimental.pallas import tpu as pltpu
from jax.sharding import PartitionSpec as P

PANEL_WIDTH = 512
BLOCK = 128
TILE_WIDTH = 64
LEAD = 2 * PANEL_WIDTH
LEAD_BLOCKS = LEAD // BLOCK
ROWS = 8
Z = 8
X = 4
PIECE = 256

HIGHEST = lax.Precision.HIGHEST
ANY = pl.BlockSpec(memory_space=pl.ANY)
VMEM = pl.BlockSpec(memory_space=pltpu.VMEM)
MIB = 1024 * 1024


def dot(a, b, dims=((1,), (0,)), precision=HIGHEST):
    return lax.dot_general(
        a, b, (dims, ((), ())), precision=precision, preferred_element_type=jnp.float32
    )


def position():
    me = lax.axis_index("blk")
    return me // (X * Z), me // Z % X, me % Z


def device(y, x, z):
    return {"blk": (y * X + lax.rem(x + X, X)) * Z + lax.rem(z + Z, Z)}


def remote(src, dst, send, recv, target):
    return pltpu.make_async_remote_copy(
        src_ref=src,
        dst_ref=dst,
        send_sem=send,
        recv_sem=recv,
        device_id=target,
        device_id_type=pl.DeviceIdType.MESH,
    )


def greet(partners):
    barrier = pltpu.get_barrier_semaphore()
    for partner in partners:
        pl.semaphore_signal(
            barrier, inc=1, device_id=partner, device_id_type=pl.DeviceIdType.MESH
        )
    pl.semaphore_wait(barrier, len(partners))


def pieces_of(s):
    edges = [s * BLOCK] + [c for c in range(PIECE, LEAD + 1, PIECE) if c > s * BLOCK]
    return list(zip(edges[:-1], edges[1:]))


def share_kernel(own_ref, out_ref, local_sem, z_send, a_send, recv):
    y, x, z = position()
    greet(
        [
            device(1 - y, x, z),
            device(y, x - 1, z),
            device(y, x + 1, z),
            device(y, x, z - 1),
            device(y, x, z + 1),
        ]
    )
    root = (y == 0) & (x == 0)

    @pl.when(root)
    def _():
        copy = pltpu.make_async_copy(own_ref, out_ref.at[z], local_sem)
        copy.start()
        copy.wait()

    def piece(s, p, send, target):
        c0, c1 = pieces_of(s)[p]
        part = out_ref.at[s, :, c0:c1]
        return remote(part, part, send, recv.at[s, p], target)

    def tree_sends(s, p):
        onward = (x == 1) if p % 2 == 0 else (x == 3)
        step = 1 if p % 2 == 0 else -1
        return [
            (root, piece(s, p, a_send.at[p, 0], device(1, x, z))),
            (x == 0, piece(s, p, a_send.at[p, 1], device(y, x + 1, z))),
            (x == 0, piece(s, p, a_send.at[p, 2], device(y, x - 1, z))),
            (onward, piece(s, p, a_send.at[p, 3], device(y, x + step, z))),
        ]

    def up_hops(s):
        return 4 if s % 2 == 0 else 3

    def ring_sends(s, p, away):
        ups = up_hops(s)
        go_up = away < ups
        go_down = (away == 0) | (away > ups + 1)
        return [
            (go_up, piece(s, p, z_send.at[s, p, 0], device(y, x, z + 1))),
            (go_down, piece(s, p, z_send.at[s, p, 1], device(y, x, z - 1))),
        ]

    def start(sends):
        for condition, copy in sends:
            pl.when(condition)(copy.start)

    def arrived(s, p):
        piece(s, p, z_send.at[s, p, 0], device(y, x, z + 1)).wait_recv()

    for s in range(LEAD_BLOCKS):

        @pl.when(z == s)
        def _(s=s):
            for p in range(len(pieces_of(s))):
                pl.when(jnp.logical_not(root))(lambda p=p: arrived(s, p))
                start(tree_sends(s, p))
                start(ring_sends(s, p, 0))

    def hop(t, carry):
        away = jnp.where(t % 2 == 1, (t + 1) // 2, Z - t // 2)
        for s in range(LEAD_BLOCKS):

            @pl.when(lax.rem(z - away + Z, Z) == s)
            def _(s=s):
                for p in range(len(pieces_of(s))):
                    arrived(s, p)
                    start(ring_sends(s, p, away))

        return carry

    lax.fori_loop(1, Z, hop, 0)

    for s in range(LEAD_BLOCKS):
        away = lax.rem(z - s + Z, Z)
        for p in range(len(pieces_of(s))):
            for condition, copy in ring_sends(s, p, away):
                pl.when(condition)(copy.wait_send)
            for condition, copy in tree_sends(s, p):
                pl.when(condition & (away == 0))(copy.wait_send)


def share(own):
    most = LEAD // PIECE
    return pl.pallas_call(
        share_kernel,
        out_shape=jax.ShapeDtypeStruct((LEAD_BLOCKS, BLOCK, LEAD), jnp.float32),
        in_specs=[ANY],
        out_specs=VMEM,
        scratch_shapes=[
            pltpu.SemaphoreType.DMA,
            pltpu.SemaphoreType.DMA((LEAD_BLOCKS, most, 2)),
            pltpu.SemaphoreType.DMA((most, 4)),
            pltpu.SemaphoreType.DMA((LEAD_BLOCKS, most)),
        ],
        compiler_params=pltpu.CompilerParams(
            collective_id=0, has_side_effects=True, vmem_limit_bytes=16 * MIB
        ),
        name="share",
    )(own)


def spread_out(x):
    return jnp.broadcast_to(x, (ROWS, BLOCK))


def refined_rsqrt(d):
    guess = lax.rsqrt(d)
    return guess * (1.5 - 0.5 * d * guess * guess)


def eliminate(parts, low, inv):
    done = []
    for r in range(ROWS):
        value = parts[r]
        for s in range(r):
            value = value - low[r][s] * done[s]
        done.append(value * inv[r])
    return done


def small_factor(cols):
    a = [[spread_out(cols[s][r : r + 1, :]) for s in range(r + 1)] for r in range(ROWS)]
    low = [[None] * ROWS for _ in range(ROWS)]
    inv = [None] * ROWS
    for s in range(ROWS):
        inv[s] = refined_rsqrt(a[s][s])
        for r in range(s + 1, ROWS):
            low[r][s] = a[r][s] * inv[s]
        for r in range(s + 1, ROWS):
            for t in range(s + 1, r + 1):
                a[r][t] = a[r][t] - low[r][s] * low[t][s]
    return low, inv


def invert_factor(a_ref, x_ref):
    row = lax.broadcasted_iota(jnp.int32, (BLOCK, BLOCK), 0)
    col = lax.broadcasted_iota(jnp.int32, (BLOCK, BLOCK), 1)
    x_ref[...] = jnp.where(row == col, 1.0, 0.0).astype(jnp.float32)
    for j in range(0, BLOCK, ROWS):
        w = a_ref[j : j + ROWS, :]
        e = x_ref[j : j + ROWS, :]
        low, inv = small_factor([spread_out(w[:, j + s : j + s + 1]) for s in range(ROWS)])
        y = eliminate([spread_out(w[r : r + 1, :]) for r in range(ROWS)], low, inv)
        f = eliminate([spread_out(e[r : r + 1, :]) for r in range(ROWS)], low, inv)
        for r in range(ROWS):
            x_ref[j + r : j + r + 1, :] = f[r][0:1, :]
        for i in range(j + ROWS, BLOCK, ROWS):
            block = a_ref[i : i + ROWS, :]
            other = x_ref[i : i + ROWS, :]
            z = eliminate(
                [spread_out(block[:, j + s : j + s + 1]) for s in range(ROWS)], low, inv
            )
            for s in range(ROWS):
                block = block - z[s] * y[s]
                other = other - z[s] * f[s]
            a_ref[i : i + ROWS, :] = block
            x_ref[i : i + ROWS, :] = other


def factor_kernel(index_ref, lead_ref, own_ref, l_ref, work, a_ref, x_ref):
    width = LEAD + BLOCK
    for s in range(LEAD_BLOCKS):
        work[s, :, 0:LEAD] = lead_ref[s]
        work[s, :, LEAD:width] = own_ref[:, s * BLOCK : (s + 1) * BLOCK].T
    per_panel = PANEL_WIDTH // BLOCK

    def step(b, carry):
        a_ref[...] = work[b, :, pl.ds(pl.multiple_of(b * BLOCK, BLOCK), BLOCK)]
        invert_factor(a_ref, x_ref)
        work[b] = dot(x_ref[...], work[b])

        def update(t, carry):
            crossing = work[b, :, pl.ds(pl.multiple_of(t * BLOCK, BLOCK), BLOCK)]
            work[t] = work[t] - dot(crossing, work[b], ((0,), (0,)))
            return carry

        lax.fori_loop(b + 1, (b // per_panel + 1) * per_panel, update, 0)

        @pl.when(b == per_panel - 1)
        def _():
            first = work[0:per_panel, :, PANEL_WIDTH:width].astype(jnp.bfloat16)
            first = first.reshape(PANEL_WIDTH, width - PANEL_WIDTH)
            for t in range(per_panel):
                rows = work[per_panel + t, :, PANEL_WIDTH:width]
                crossing = first[:, t * BLOCK : (t + 1) * BLOCK]
                work[per_panel + t, :, PANEL_WIDTH:width] = rows - dot(
                    crossing, first, ((0,), (0,)), None
                )

        return carry

    lax.fori_loop(0, LEAD_BLOCKS, step, 0)
    for s in range(LEAD_BLOCKS):
        q = lax.broadcasted_iota(jnp.int32, (BLOCK, BLOCK), 0) + s * BLOCK
        c = lax.broadcasted_iota(jnp.int32, (BLOCK, BLOCK), 1) + index_ref[0] * BLOCK
        own = jnp.where(q <= c, work[s, :, LEAD:width], 0.0)
        l_ref[:, s * BLOCK : (s + 1) * BLOCK] = own.T.astype(jnp.bfloat16)


def factor(index, lead, own):
    return pl.pallas_call(
        factor_kernel,
        out_shape=jax.ShapeDtypeStruct((BLOCK, LEAD), jnp.bfloat16),
        in_specs=[pl.BlockSpec(memory_space=pltpu.SMEM), VMEM, VMEM],
        out_specs=VMEM,
        scratch_shapes=[
            pltpu.VMEM((LEAD_BLOCKS, BLOCK, LEAD + BLOCK), jnp.float32),
            pltpu.VMEM((BLOCK, BLOCK), jnp.float32),
            pltpu.VMEM((BLOCK, BLOCK), jnp.float32),
        ],
        compiler_params=pltpu.CompilerParams(vmem_limit_bytes=32 * MIB),
        name="factor",
    )(index, lead, own)


def exchange_kernel(
    l_ref, q_ref, line, plane, made, local_sem, l_send, l_recv, p_send, p_recv, q_send, q_recv
):
    y, x, z = position()
    a = y * X + x
    A = 2 * X
    others = [lax.rem(a + i, A) for i in range(1, A)]
    greet(
        [device(y, x, z - 1), device(y, x, z + 1)]
        + [device(other // X, other % X, z) for other in others]
    )

    def rows(index, half=None):
        if half is None:
            return pl.ds(pl.multiple_of(lax.rem(index + Z, Z) * BLOCK, BLOCK), BLOCK)
        start = lax.rem(index + Z, Z) * BLOCK + half * (BLOCK // 2)
        return pl.ds(pl.multiple_of(start, BLOCK // 2), BLOCK // 2)

    own_line = pltpu.make_async_copy(l_ref, line.at[rows(z)], local_sem.at[0])
    own_plane = pltpu.make_async_copy(l_ref, plane.at[rows(a)], local_sem.at[1])
    own_line.start()
    own_plane.start()

    def line_copy(up, hop):
        sign = 1 if up else -1
        half = None if hop < Z // 2 else (0 if up else 1)
        part = line.at[rows(z - sign * (hop - 1), half)]
        at = 0 if up else 1
        return remote(
            part, part, l_send.at[at, hop - 1], l_recv.at[at, hop - 1], device(y, x, z + sign)
        )

    def line_arrival(up, hop):
        sign = 1 if up else -1
        half = None if hop < Z // 2 else (0 if up else 1)
        part = line.at[rows(z - sign * hop, half)]
        at = 0 if up else 1
        return remote(
            part, part, l_send.at[at, hop - 1], l_recv.at[at, hop - 1], device(y, x, z + sign)
        )

    def plane_copy(slot, yy, source, half, target):
        part = plane.at[rows(yy * X + lax.rem(source + X, X), half)]
        return remote(part, part, p_send.at[slot], p_recv.at[slot], target)

    far = 1 - y
    right, left = device(y, x + 1, z), device(y, x - 1, z)
    over = device(far, x, z)
    sends = [
        plane_copy(0, y, x, None, over),
        plane_copy(1, y, x, None, right),
        plane_copy(2, y, x, None, left),
        plane_copy(3, far, x, None, right),
        plane_copy(4, far, x, None, left),
        plane_copy(5, y, x - 1, 0, right),
        plane_copy(6, y, x + 1, 1, left),
        plane_copy(7, far, x - 1, 0, right),
        plane_copy(8, far, x + 1, 1, left),
    ]
    arrivals = [
        plane_copy(0, far, x, None, over),
        plane_copy(1, y, x - 1, None, right),
        plane_copy(2, y, x + 1, None, left),
        plane_copy(3, far, x - 1, None, right),
        plane_copy(4, far, x + 1, None, left),
        plane_copy(5, y, x - 2, 0, right),
        plane_copy(6, y, x + 2, 1, left),
        plane_copy(7, far, x - 2, 0, right),
        plane_copy(8, far, x + 2, 1, left),
    ]
    own_line.wait()
    for up in (True, False):
        line_copy(up, 1).start()
    own_plane.wait()
    for slot in (0, 1, 2):
        sends[slot].start()

    def pass_on(hop):
        for up in (True, False):
            line_arrival(up, hop).wait_recv()
            line_copy(up, hop + 1).start()

    pass_on(1)
    arrivals[0].wait_recv()
    sends[3].start()
    sends[4].start()
    arrivals[1].wait_recv()
    sends[5].start()
    arrivals[2].wait_recv()
    sends[6].start()
    pass_on(2)
    arrivals[3].wait_recv()
    sends[7].start()
    arrivals[4].wait_recv()
    sends[8].start()
    pass_on(3)
    for slot in (5, 6, 7, 8):
        arrivals[slot].wait_recv()
    for up in (True, False):
        line_arrival(up, Z // 2).wait_recv()

    def product(other):
        j = lax.broadcasted_iota(jnp.int32, (BLOCK, LEAD), 0) + z * BLOCK
        q = lax.broadcasted_iota(jnp.int32, (BLOCK, LEAD), 1)
        chosen = jnp.where(j == q, 1.0, 0.0).astype(jnp.bfloat16)
        is_lead = jnp.full((BLOCK, LEAD), other, jnp.int32) == 0
        left_side = jnp.where(is_lead, chosen, plane[rows(other)])
        return dot(left_side, line[...], ((1,), (1,)), None)

    def part_of(index):
        return pl.ds(pl.multiple_of(index * LEAD, LEAD), LEAD)

    def product_copy(i):
        other = lax.rem(a + i, A)
        return remote(
            made.at[i],
            q_ref.at[:, part_of(a)],
            q_send.at[i],
            q_recv.at[i],
            device(other // X, lax.rem(other, X), z),
        )

    def make(i, carry):
        made[i] = product(lax.rem(a + i, A))

        @pl.when(i > 1)
        def _():
            product_copy(i - 1).start()

        return carry

    lax.fori_loop(1, A, make, 0)
    q_ref[:, part_of(a)] = product(a)
    product_copy(A - 1).start()
    for i in range(1, A):
        product_copy(i).wait()
    for up in (True, False):
        for hop in range(1, Z // 2 + 1):
            line_copy(up, hop).wait_send()
    for copy in sends:
        copy.wait_send()


def exchange(rows, order):
    dma = pltpu.SemaphoreType.DMA
    return pl.pallas_call(
        exchange_kernel,
        out_shape=jax.ShapeDtypeStruct((BLOCK, order), jnp.float32),
        in_specs=[ANY],
        out_specs=VMEM,
        scratch_shapes=[
            pltpu.VMEM((LEAD, LEAD), jnp.bfloat16),
            pltpu.VMEM((LEAD, LEAD), jnp.bfloat16),
            pltpu.VMEM((2 * X, BLOCK, LEAD), jnp.float32),
            dma((2,)),
            dma((2, Z // 2)),
            dma((2, Z // 2)),
            dma((9,)),
            dma((9,)),
            dma((2 * X,)),
            dma((2 * X,)),
        ],
        compiler_params=pltpu.CompilerParams(
            collective_id=1, has_side_effects=True, vmem_limit_bytes=32 * MIB
        ),
        name="exchange",
    )(rows)


def from_behind(shard, by):
    count = lax.axis_size("blk")
    return lax.ppermute(shard, "blk", [(i, (i + by) % count) for i in range(count)])


def contribution(tiles, places, own_places):
    slots = jnp.arange(BLOCK, dtype=jnp.int32)
    row_table = (places[..., None] == slots).astype(jnp.float32)
    shaped = tiles.reshape(TILE_WIDTH, -1, TILE_WIDTH)
    spread = jnp.einsum("cei,eiq->ceq", shaped, row_table, precision=HIGHEST)
    column_table = (own_places[..., None] == slots).astype(jnp.float32)
    return jnp.einsum(
        "cq,cn->qn", column_table, spread.reshape(TILE_WIDTH, -1), precision=HIGHEST
    )


def on_device(front, child, index_map):
    cycle = lax.axis_size("blk")
    half = cycle // 2
    index = lax.axis_index("blk")
    front, child = front[0], child[0]
    order = front.shape[1]
    places = (index_map % BLOCK).reshape(cycle, TILE_WIDTH)
    own_places = lax.dynamic_index_in_dim(places, (index - half) % cycle, 0, keepdims=False)
    early = slice(half * TILE_WIDTH, (half + LEAD_BLOCKS) * TILE_WIDTH)
    early_tiles = from_behind(child[:, early], half)
    own = front[:, :LEAD] + contribution(
        early_tiles, places[half : half + LEAD_BLOCKS], own_places
    )
    lead = share(own)
    lead, child = lax.optimization_barrier((lead, child))
    tiles = from_behind(child, half)
    rows = factor(index[None].astype(jnp.int32), lead, own)
    product = exchange(rows, order)
    middle = half * TILE_WIDTH
    tiles = jnp.concatenate([tiles[:, middle:], tiles[:, :middle]], axis=1)
    added = contribution(tiles, jnp.concatenate([places[half:], places[:half]]), own_places)
    remaining = jnp.where(jnp.arange(order) < LEAD, 0.0, front + added - product)
    return jnp.where(index < LEAD_BLOCKS, product, remaining)[None]


def solution(mesh):
    placed = (P("front", "blk", None), P("front", "blk", None), P("front"))
    return jax.shard_map(
        on_device, mesh=mesh, in_specs=placed, out_specs=P("front", "blk", None), check_vma=False
    )
```

time: 730 us -> 222 us (0.30)
  waiting for transfers between devices: 277 us -> 3.53 us
  other arithmetic: 242 us -> 0.81 us
  Pallas kernels: 0 us -> 183 us
  blocking collectives: 98.4 us -> 0 us
  local copies, waits for them, and re-layouts: 34.3 us -> 8.53 us
  matrix products: 34.4 us -> 12 us
  between operations: 19.6 us -> 0.16 us
    another operation x35 -> x0, other arithmetic: 238 us -> none  [the longest x15 79.5 us: on_device(): jnp.linalg.cholesky(second_diag)]
    pallas_call x0 -> x3, Pallas kernels: none -> 183 us  [the longest x1 86.7 us: exchange(): pl.pallas_call(exchange_kernel, out_shape=jax.ShapeDtypeStruct((BLOCK, or...]
    all_gather x1 -> x0, waiting for transfers between devices: 180 us -> none  [on_device(): lax.all_gather(lowered, 'blk', axis=0, tiled=True)]
    all_to_all x2 -> x0, blocking collectives: 98.4 us -> none  [sent_and_summed(): pieces = lax.all_to_all(split_up(shard, dim, count), axis, 0, 0, tiled=True)]
    all_to_all x2 -> x0, waiting for transfers between devices: 73.3 us -> none  [from_everyone(): return lax.all_to_all(copies, axis, split_axis=0, concat_axis=0, tiled=True)]
    ppermute x1 -> x2, waiting for transfers between devices: 23.4 us -> 3.53 us  [from_behind(): lax.ppermute(shard, 'blk', [(i, (i + by) % count) for i in range(count)])]
    another operation x38 -> x0, local copies, waits for them, and re-layouts: 18.3 us -> none  [the longest x27 16 us: own_rows(): lax.linalg.triangular_solve(diag_factor, panel_part, left_side=False, low...]
    all_to_all x2 -> x0, starting transfers between devices: 14.1 us -> none  [from_everyone(): return lax.all_to_all(copies, axis, split_axis=0, concat_axis=0, tiled=True)]
  transfers between devices with their start and end apart: 4 -> 2, of which waited for: 4 -> 1; matrix products, arithmetic and copies ran while one was open for 1% -> 0% of each run, Pallas kernels for 0% -> 65%
where the time goes in v1:
time: 222 us; the launch traced here: 218 us
  Pallas kernels  183 us (82%)
  matrix products  12 us (5%)
  starting transfers between devices  9.4 us (4%)
  local copies, waits for them, and re-layouts  8.53 us (4%)
  waiting for transfers between devices  3.53 us (2%)
    pallas_call x1, Pallas kernels, exchange(): pl.pallas_call(exchange_kernel, out_shape=jax.ShapeDtypeStruct((BLOCK, or...  86.7 us
    pallas_call x1, Pallas kernels, factor(): pl.pallas_call(factor_kernel, out_shape=jax.ShapeDtypeStruct((BLOCK, LEAD...  53.7 us
    pallas_call x1, Pallas kernels, share(): pl.pallas_call(share_kernel, out_shape=jax.ShapeDtypeStruct((LEAD_BLOCKS,...  42.8 us
    ppermute x2, starting transfers between devices, from_behind(): lax.ppermute(shard, 'blk', [(i, (i + by) % count) for i in range(count)])  9.4 us
    dot_general x2, matrix products, contribution(): jnp.einsum('cq,cn->qn', column_table, spread.reshape(TILE_WIDTH, -1), pre...  8.27 us
    unnamed x10, local copies, waits for them, and re-layouts  6.21 us
  transfers between devices with their start and end apart: 2, of which 1 were waited for; matrix products, arithmetic and copies ran while one was open for 0% of the time, Pallas kernels for 65%

profile of v1, /device:TPU:8, one launch (start us, length us, event | category | flops | bytes accessed | tf_op | source)
XLA Modules:
  0.0 217.6 jit_solution(10800448780148742884)
XLA Ops:
  0.0 0.0 copy-start.4
  0.0 1.0 slice.66
  1.0 2.4 %collective-permute-start = (f32[64,512]{1,0:T(8,128)S(1)}, f32[64,512]{1,0:T(8,128)S(1)}, u32[]{:S(2)}, u32[]{:S(2)}) collective-permute-start(f32[64,512]{1,0:T(8,128)S(1)} %slice.66), channel_id=1, source_target_pairs={{0,32},{1,33},{2,34},{3,35},{4,36},{5,37},{6,38},{7,39},{8,40},{9,... | collective-permute-start | bytes 393224 | tf_op jit(solution)/shard_map/ppermute | solution.py:454
  3.4 0.7 add_select_fusion
  4.2 0.1 reshape.47
  4.2 0.1 slice.56
  4.3 3.5 %collective-permute-done = f32[64,512]{1,0:T(8,128)S(1)} collective-permute-done((f32[64,512]{1,0:T(8,128)S(1)}, f32[64,512]{1,0:T(8,128)S(1)}, u32[]{:S(2)}, u32[]{:S(2)}) %collective-permute-start) | collective-permute-done | bytes 131104 | tf_op jit(solution)/shard_map/ppermute | solution.py:454
  7.8 0.1 reshape.48
  7.9 0.3 convolution_bitcast_fusion
  8.3 1.5 convolution_add_fusion.1.own_ref
  9.8 42.8 %share.1.lead_ref = f32[8,128,1024]{2,1,0:T(8,128)S(1)} custom-call(f32[128,1024]{1,0:T(8,128)S(1)} %convolution_add_fusion.1.own_ref), custom_call_target="tpu_custom_call" | custom-call | tf_op jit(solution)/shard_map/share/pallas_call | solution.py:151
  52.6 0.0 copy-start
  52.6 2.0 copy-done
  54.6 0.0 copy-done.4
  54.6 7.0 %collective-permute-start.1 = (f32[64,4096]{1,0:T(8,128)S(1)}, f32[64,4096]{1,0:T(8,128)S(1)}, u32[]{:S(2)}, u32[]{:S(2)}) collective-permute-start(f32[64,4096]{1,0:T(8,128)S(1)} %bitcast.22), channel_id=1, source_target_pairs={{0,32},{1,33},{2,34},{3,35},{4,36},{5,37},{6,38},{7,39},{8,40},{9,... | collective-permute-start | bytes 3145736 | tf_op jit(solution)/shard_map/ppermute | solution.py:454
  61.6 0.1 slice.59
  61.7 0.1 slice.61
  61.8 0.0 copy-start.1
  61.8 2.2 %copy-done.1 = f32[8,128,1024]{2,1,0:T(8,128)S(1)} copy-done((f32[8,128,1024]{2,1,0:T(8,128)S(1)}, f32[8,128,1024]{2,1,0:T(8,128)}, u32[]{:S(2)}) %copy-start.1) | copy-done | bytes 4194328
  64.0 53.7 %factor.1.l_ref = bf16[128,1024]{1,0:T(8,128)(2,1)S(1)} custom-call(s32[1]{0:T(128)} %bitcast.index_ref, f32[8,128,1024]{2,1,0:T(8,128)S(1)} %copy-done.1, f32[128,1024]{1,0:T(8,128)S(1)} %convolution_add_fusion.1.own_ref), custom_call_target="tpu_custom_call" | custom-call | tf_op jit(solution)/shard_map/factor/pallas_call | solution.py:268
  117.7 86.7 %exchange.1 = f32[128,8192]{1,0:T(8,128)S(1)} custom-call(bf16[128,1024]{1,0:T(8,128)(2,1)S(1)} %factor.1.l_ref), custom_call_target="tpu_custom_call" | custom-call | tf_op jit(solution)/shard_map/exchange/pallas_call | solution.py:428
  204.4 0.0 copy-start.2
  204.4 2.0 copy-done.2
  206.4 0.0 collective-permute-done.1
  206.4 0.1 fusion.19
  206.5 0.1 pad_maximum_fusion
  206.6 0.8 reshape.50
  207.4 0.0 copy-start.3
  207.4 3.4 %fusion.8 = f32[64,8,8,128]{3,2,1,0:T(8,128)S(1)} fusion(f32[64,64,64]{2,1,0:T(8,128)S(1)} %reshape.50, s32[64,64]{1,0:T(8,128)S(1)} %pad_add_fusion), kind=kOutput, calls=%fused_computation.10 | convolution fusion | flops 403177472 | bytes 3162112 | tf_op jit(solution)/shard_map/cei,eiq->ceq/dot_general | solution.py:461
  210.8 0.0 copy-done.3
  210.8 6.7 %fusion.3 = f32[1,128,8192]{2,1,0:T(8,128)} fusion(f32[128,8192]{1,0:T(8,128)S(1)} %copy-done.3, f32[64,8,8,128]{3,2,1,0:T(8,128)S(1)} %fusion.8, pred[8192]{0:T(1024)(128)(4,1)S(1)} %iota_compare_fusion.6, pred[]{:T(512)S(6)} %lt.25, s32[64]{0:T(128)S(1)} %dynamic-slice_bitcast_fusion, f32[1,128,8192]{2,1,0:T(8,128)} %param.3), kind=kOutput, calls=%fused_computation.4 | convolution fusion | flops 809508864 | bytes 14688513 | tf_op jit(solution)/shard_map/cq,cn->qn/dot_general | solution.py:463
  (5 shorter events, 0.0 us)
Async XLA Ops:
  0.0 54.6 %copy-start.4 = (f32[1,64,4096]{2,1,0:T(8,128)S(1)}, f32[1,64,4096]{2,1,0:T(8,128)}, u32[]{:S(2)}) copy-start(f32[1,64,4096]{2,1,0:T(8,128)} %param.4) | copy-start | bytes 3145732
  1.0 6.8 %collective-permute-start = (f32[64,512]{1,0:T(8,128)S(1)}, f32[64,512]{1,0:T(8,128)S(1)}, u32[]{:S(2)}, u32[]{:S(2)}) collective-permute-start(f32[64,512]{1,0:T(8,128)S(1)} %slice.66), channel_id=1, source_target_pairs={{0,32},{1,33},{2,34},{3,35},{4,36},{5,37},{6,38},{7,39},{8,40},{9,... | collective-permute-start | bytes 393224 | tf_op jit(solution)/shard_map/ppermute | solution.py:454
  52.6 2.0 copy-start
  54.6 151.8 %collective-permute-start.1 = (f32[64,4096]{1,0:T(8,128)S(1)}, f32[64,4096]{1,0:T(8,128)S(1)}, u32[]{:S(2)}, u32[]{:S(2)}) collective-permute-start(f32[64,4096]{1,0:T(8,128)S(1)} %bitcast.22), channel_id=1, source_target_pairs={{0,32},{1,33},{2,34},{3,35},{4,36},{5,37},{6,38},{7,39},{8,40},{9,... | collective-permute-start | bytes 3145736 | tf_op jit(solution)/shard_map/ppermute | solution.py:454
  61.8 2.2 %copy-start.1 = (f32[8,128,1024]{2,1,0:T(8,128)S(1)}, f32[8,128,1024]{2,1,0:T(8,128)}, u32[]{:S(2)}) copy-start(f32[8,128,1024]{2,1,0:T(8,128)} %copy-done) | copy-start | bytes 12582916
  204.4 2.0 copy-start.2
  207.4 3.4 %copy-start.3 = (f32[128,8192]{1,0:T(8,128)S(1)}, f32[128,8192]{1,0:T(8,128)}, u32[]{:S(2)}) copy-start(f32[128,8192]{1,0:T(8,128)} %copy-done.2) | copy-start | bytes 12582916

commit v2 on v1

--- a/solution.py
+++ b/solution.py
@@ -280,173 +280,247 @@
     )(index, lead, own)
 
 
+STEPS = 2 * X
+
+
 def exchange_kernel(
-    l_ref, q_ref, line, plane, made, local_sem, l_send, l_recv, p_send, p_recv, q_send, q_recv
+    l_ref, front_ref, tiles_ref, places_ref, index_ref, out_ref,
+    line, plane, made, came, z_made, z_came, picked,
+    local_sem, l_send, l_recv, p_send, p_recv, q_send, q_recv, z_send, z_recv,
 ):
     y, x, z = position()
     a = y * X + x
-    A = 2 * X
-    others = [lax.rem(a + i, A) for i in range(1, A)]
-    greet(
-        [device(y, x, z - 1), device(y, x, z + 1)]
-        + [device(other // X, other % X, z) for other in others]
-    )
-
-    def rows(index, half=None):
+    up, down = device(y, x, z + 1), device(y, x, z - 1)
+    right, left, over = device(y, x + 1, z), device(y, x - 1, z), device(1 - y, x, z)
+
+    def plane_index(slot):
+        return lax.rem(y + slot // X, 2) * X + lax.rem(x + lax.rem(slot, X), X)
+
+    def plane_device(slot):
+        return {"blk": plane_index(slot) * Z + z}
+
+    greet([up, down] + [plane_device(slot) for slot in range(1, STEPS)])
+
+    def rows(slot, half=None):
         if half is None:
-            return pl.ds(pl.multiple_of(lax.rem(index + Z, Z) * BLOCK, BLOCK), BLOCK)
-        start = lax.rem(index + Z, Z) * BLOCK + half * (BLOCK // 2)
-        return pl.ds(pl.multiple_of(start, BLOCK // 2), BLOCK // 2)
-
-    own_line = pltpu.make_async_copy(l_ref, line.at[rows(z)], local_sem.at[0])
-    own_plane = pltpu.make_async_copy(l_ref, plane.at[rows(a)], local_sem.at[1])
+            return pl.ds(slot * BLOCK, BLOCK)
+        return pl.ds(slot * BLOCK + half * (BLOCK // 2), BLOCK // 2)
+
+    own_line = pltpu.make_async_copy(l_ref, line.at[rows(0)], local_sem.at[0])
+    own_plane = pltpu.make_async_copy(l_ref, plane.at[rows(0)], local_sem.at[1])
+    base = pltpu.make_async_copy(front_ref, out_ref, local_sem.at[2])
     own_line.start()
     own_plane.start()
-
-    def line_copy(up, hop):
-        sign = 1 if up else -1
-        half = None if hop < Z // 2 else (0 if up else 1)
-        part = line.at[rows(z - sign * (hop - 1), half)]
-        at = 0 if up else 1
+    base.start()
+
+    def line_copy(way, hop):
+        half = None if hop < Z // 2 else way
+        sign = -1 if way == 0 else 1
+        start, end = (sign * (hop - 1)) % Z, (sign * hop) % Z
         return remote(
-            part, part, l_send.at[at, hop - 1], l_recv.at[at, hop - 1], device(y, x, z + sign)
+            line.at[rows(start, half)],
+            line.at[rows(end, half)],
+            l_send.at[way, hop - 1],
+            l_recv.at[way, hop - 1],
+            up if way == 0 else down,
         )
 
-    def line_arrival(up, hop):
-        sign = 1 if up else -1
-        half = None if hop < Z // 2 else (0 if up else 1)
-        part = line.at[rows(z - sign * hop, half)]
-        at = 0 if up else 1
+    def plane_copy(number, start, end, half, target):
         return remote(
-            part, part, l_send.at[at, hop - 1], l_recv.at[at, hop - 1], device(y, x, z + sign)
+            plane.at[rows(start, half)],
+            plane.at[rows(end, half)],
+            p_send.at[number],
+            p_recv.at[number],
+            target,
         )
 
-    def plane_copy(slot, yy, source, half, target):
-        part = plane.at[rows(yy * X + lax.rem(source + X, X), half)]
-        return remote(part, part, p_send.at[slot], p_recv.at[slot], target)
-
-    far = 1 - y
-    right, left = device(y, x + 1, z), device(y, x - 1, z)
-    over = device(far, x, z)
-    sends = [
-        plane_copy(0, y, x, None, over),
-        plane_copy(1, y, x, None, right),
-        plane_copy(2, y, x, None, left),
-        plane_copy(3, far, x, None, right),
-        plane_copy(4, far, x, None, left),
-        plane_copy(5, y, x - 1, 0, right),
-        plane_copy(6, y, x + 1, 1, left),
-        plane_copy(7, far, x - 1, 0, right),
-        plane_copy(8, far, x + 1, 1, left),
-    ]
-    arrivals = [
-        plane_copy(0, far, x, None, over),
-        plane_copy(1, y, x - 1, None, right),
-        plane_copy(2, y, x + 1, None, left),
-        plane_copy(3, far, x - 1, None, right),
-        plane_copy(4, far, x + 1, None, left),
-        plane_copy(5, y, x - 2, 0, right),
-        plane_copy(6, y, x + 2, 1, left),
-        plane_copy(7, far, x - 2, 0, right),
-        plane_copy(8, far, x + 2, 1, left),
+    across = [
+        plane_copy(0, 0, 4, None, over),
+        plane_copy(1, 0, 3, None, right),
+        plane_copy(2, 0, 1, None, left),
+        plane_copy(3, 4, 7, None, right),
+        plane_copy(4, 4, 5, None, left),
+        plane_copy(5, 3, 2, 0, right),
+        plane_copy(6, 1, 2, 1, left),
+        plane_copy(7, 7, 6, 0, right),
+        plane_copy(8, 5, 6, 1, left),
     ]
     own_line.wait()
-    for up in (True, False):
-        line_copy(up, 1).start()
+    line_copy(0, 1).start()
+    line_copy(1, 1).start()
     own_plane.wait()
-    for slot in (0, 1, 2):
-        sends[slot].start()
+    for number in (0, 1, 2):
+        across[number].start()
+
+    slot_of = lax.broadcasted_iota(jnp.int32, (BLOCK, TILE_WIDTH), 0)
+    column_table = jnp.where(slot_of == places_ref[...], 1.0, 0.0).astype(jnp.float32)
+    order = picked.shape[1]
+    for start in range(0, order, LEAD):
+        picked[:, start : start + LEAD] = dot(column_table, tiles_ref[:, start : start + LEAD])
+    pairs = order // BLOCK
+
+    def place(pair, carry):
+        start = lax.rem(pair + pairs // 2, pairs) * (2 * BLOCK)
+        slot = lax.broadcasted_iota(jnp.int32, (2 * BLOCK, BLOCK), 0) + start
+        row_table = jnp.where(slot == index_ref[pl.ds(pair, 1), :], 1.0, 0.0).astype(jnp.float32)
+        part = picked[:, pl.ds(pl.multiple_of(pair * BLOCK, BLOCK), BLOCK)]
+        columns = pl.ds(pl.multiple_of(start, BLOCK), 2 * BLOCK)
+        out_ref[:, columns] = out_ref[:, columns] + dot(part, row_table, ((1,), (1,)))
+        return carry
 
     def pass_on(hop):
-        for up in (True, False):
-            line_arrival(up, hop).wait_recv()
-            line_copy(up, hop + 1).start()
+        for way in (0, 1):
+            line_copy(way, hop).wait_recv()
+            line_copy(way, hop + 1).start()
+
+    def pass_across(number, *onward):
+        across[number].wait_recv()
+        for other in onward:
+            across[other].start()
 
     pass_on(1)
-    arrivals[0].wait_recv()
-    sends[3].start()
-    sends[4].start()
-    arrivals[1].wait_recv()
-    sends[5].start()
-    arrivals[2].wait_recv()
-    sends[6].start()
+    pass_across(0, 3, 4)
+    pass_across(1, 5)
+    pass_across(2, 6)
+    base.wait()
+    lax.fori_loop(0, pairs // 4, place, 0)
     pass_on(2)
-    arrivals[3].wait_recv()
-    sends[7].start()
-    arrivals[4].wait_recv()
-    sends[8].start()
+    pass_across(3, 7)
+    pass_across(4, 8)
+    lax.fori_loop(pairs // 4, pairs // 2, place, 0)
     pass_on(3)
-    for slot in (5, 6, 7, 8):
-        arrivals[slot].wait_recv()
-    for up in (True, False):
-        line_arrival(up, Z // 2).wait_recv()
-
-    def product(other):
-        j = lax.broadcasted_iota(jnp.int32, (BLOCK, LEAD), 0) + z * BLOCK
+    lax.fori_loop(pairs // 2, pairs, place, 0)
+    for number in (5, 6, 7, 8):
+        pass_across(number)
+    for way in (0, 1):
+        line_copy(way, Z // 2).wait_recv()
+
+    def lefts(block, holder, zz):
+        j = lax.broadcasted_iota(jnp.int32, (BLOCK, LEAD), 0) + lax.rem(zz + Z, Z) * BLOCK
         q = lax.broadcasted_iota(jnp.int32, (BLOCK, LEAD), 1)
         chosen = jnp.where(j == q, 1.0, 0.0).astype(jnp.bfloat16)
-        is_lead = jnp.full((BLOCK, LEAD), other, jnp.int32) == 0
-        left_side = jnp.where(is_lead, chosen, plane[rows(other)])
-        return dot(left_side, line[...], ((1,), (1,)), None)
-
-    def part_of(index):
-        return pl.ds(pl.multiple_of(index * LEAD, LEAD), LEAD)
-
-    def product_copy(i):
-        other = lax.rem(a + i, A)
+        is_lead = jnp.full((BLOCK, LEAD), holder, jnp.int32) == 0
+        return jnp.where(is_lead, chosen, block)
+
+    def product(left_side, right_side):
+        return dot(left_side, right_side, ((1,), (1,)), None)
+
+    near = (2 * BLOCK, 7 * BLOCK)
+
+    def product_copy(slot):
+        landing = slot // X * X + lax.rem(X - lax.rem(slot, X), X)
         return remote(
-            made.at[i],
-            q_ref.at[:, part_of(a)],
-            q_send.at[i],
-            q_recv.at[i],
-            device(other // X, lax.rem(other, X), z),
+            made.at[slot], came.at[landing], q_send.at[slot], q_recv.at[landing], plane_device(slot)
         )
 
-    def make(i, carry):
-        made[i] = product(lax.rem(a + i, A))
-
-        @pl.when(i > 1)
+    def z_copy(way):
+        return remote(
+            z_made.at[way],
+            z_came.at[way],
+            z_send.at[way],
+            z_recv.at[way],
+            up if way == 0 else down,
+        )
+
+    sends = a != 0
+
+    def make(slot, carry):
+        block = plane[pl.ds(pl.multiple_of(slot * BLOCK, BLOCK), BLOCK)]
+        made[slot] = product(lefts(block, plane_index(slot), z), line[near[0] : near[1]])
+
+        @pl.when(sends & (slot > 1))
         def _():
-            product_copy(i - 1).start()
+            product_copy(slot - 1).start()
 
         return carry
 
-    lax.fori_loop(1, A, make, 0)
-    q_ref[:, part_of(a)] = product(a)
-    product_copy(A - 1).start()
-    for i in range(1, A):
-        product_copy(i).wait()
-    for up in (True, False):
+    lax.fori_loop(1, STEPS, make, 0)
+    z_made[0] = product(lefts(line[rows(1)], a, z + 1), plane[BLOCK:])
+    pl.when(sends)(product_copy(STEPS - 1).start)
+    z_made[1] = product(lefts(line[rows(Z - 1)], a, z - 1), plane[BLOCK:])
+    z_copy(0).start()
+
+    def put(aa, zz, value):
+        block = aa * Z + lax.rem(zz + Z, Z)
+        columns = pl.ds(pl.multiple_of(block * BLOCK, BLOCK), BLOCK)
+        kept = jnp.where(jnp.full((BLOCK, BLOCK), aa, jnp.int32) == 0, 0.0, out_ref[:, columns] - value)
+        is_lead = jnp.full((BLOCK, BLOCK), a, jnp.int32) == 0
+        out_ref[:, columns] = jnp.where(is_lead, value, kept)
+
+    own = lefts(line[rows(0)], a, z)
+    along = product(own, line[...])
+    z_copy(1).start()
+    for s in range(Z):
+        put(a, z + s, along[:, s * BLOCK : (s + 1) * BLOCK])
+    along = product(own, plane[BLOCK:])
+    for slot in range(1, STEPS):
+        put(plane_index(slot), z, along[:, (slot - 1) * BLOCK : slot * BLOCK])
+    for way in (0, 1):
+        z_copy(way).wait_recv()
+        for slot in range(1, STEPS):
+            value = z_came[way, :, (slot - 1) * BLOCK : slot * BLOCK]
+            put(plane_index(slot), z - 1 if way == 0 else z + 1, value)
+
+    def take(slot, carry):
+        source = plane_index(slot)
+
+        @pl.when(source != 0)
+        def _():
+            landing = slot // X * X + lax.rem(X - lax.rem(slot, X), X)
+            product_copy(landing).wait_recv()
+            for s in range(2, Z - 1):
+                put(source, z + s, came[slot, :, (s - 2) * BLOCK : (s - 1) * BLOCK])
+
+        @pl.when(source == 0)
+        def _():
+            for s in range(2, Z - 1):
+                columns = pl.ds(pl.multiple_of(lax.rem(z + s, Z) * BLOCK, BLOCK), BLOCK)
+                out_ref[:, columns] = jnp.zeros((BLOCK, BLOCK), jnp.float32)
+
+        return carry
+
+    lax.fori_loop(1, STEPS, take, 0)
+    for slot in range(1, STEPS):
+        pl.when(sends)(product_copy(slot).wait_send)
+    for way in (0, 1):
+        z_copy(way).wait_send()
         for hop in range(1, Z // 2 + 1):
-            line_copy(up, hop).wait_send()
-    for copy in sends:
+            line_copy(way, hop).wait_send()
+    for copy in across:
         copy.wait_send()
 
 
-def exchange(rows, order):
+def exchange(rows, front, tiles, places, index_map):
     dma = pltpu.SemaphoreType.DMA
+    f32 = jnp.float32
     return pl.pallas_call(
         exchange_kernel,
-        out_shape=jax.ShapeDtypeStruct((BLOCK, order), jnp.float32),
-        in_specs=[ANY],
+        out_shape=jax.ShapeDtypeStruct(front.shape, f32),
+        in_specs=[ANY, ANY, VMEM, VMEM, VMEM],
         out_specs=VMEM,
         scratch_shapes=[
-            pltpu.VMEM((LEAD, LEAD), jnp.bfloat16),
-            pltpu.VMEM((LEAD, LEAD), jnp.bfloat16),
-            pltpu.VMEM((2 * X, BLOCK, LEAD), jnp.float32),
-            dma((2,)),
+            pltpu.VMEM((Z * BLOCK, LEAD), jnp.bfloat16),
+            pltpu.VMEM((STEPS * BLOCK, LEAD), jnp.bfloat16),
+            pltpu.VMEM((STEPS, BLOCK, 5 * BLOCK), f32),
+            pltpu.VMEM((STEPS, BLOCK, 5 * BLOCK), f32),
+            pltpu.VMEM((2, BLOCK, 7 * BLOCK), f32),
+            pltpu.VMEM((2, BLOCK, 7 * BLOCK), f32),
+            pltpu.VMEM((BLOCK, tiles.shape[1]), f32),
+            dma((3,)),
             dma((2, Z // 2)),
             dma((2, Z // 2)),
             dma((9,)),
             dma((9,)),
-            dma((2 * X,)),
-            dma((2 * X,)),
+            dma((STEPS,)),
+            dma((STEPS,)),
+            dma((2,)),
+            dma((2,)),
         ],
         compiler_params=pltpu.CompilerParams(
-            collective_id=1, has_side_effects=True, vmem_limit_bytes=32 * MIB
+            collective_id=1, has_side_effects=True, vmem_limit_bytes=40 * MIB
         ),
         name="exchange",
-    )(rows)
+    )(rows, front, tiles, places, index_map)
 
 
 def from_behind(shard, by):
@@ -470,7 +544,6 @@
     half = cycle // 2
     index = lax.axis_index("blk")
     front, child = front[0], child[0]
-    order = front.shape[1]
     places = (index_map % BLOCK).reshape(cycle, TILE_WIDTH)
     own_places = lax.dynamic_index_in_dim(places, (index - half) % cycle, 0, keepdims=False)
     early = slice(half * TILE_WIDTH, (half + LEAD_BLOCKS) * TILE_WIDTH)
@@ -482,12 +555,7 @@
     lead, child = lax.optimization_barrier((lead, child))
     tiles = from_behind(child, half)
     rows = factor(index[None].astype(jnp.int32), lead, own)
-    product = exchange(rows, order)
-    middle = half * TILE_WIDTH
-    tiles = jnp.concatenate([tiles[:, middle:], tiles[:, :middle]], axis=1)
-    added = contribution(tiles, jnp.concatenate([places[half:], places[:half]]), own_places)
-    remaining = jnp.where(jnp.arange(order) < LEAD, 0.0, front + added - product)
-    return jnp.where(index < LEAD_BLOCKS, product, remaining)[None]
+    return exchange(rows, front, tiles, own_places[None], index_map.reshape(-1, BLOCK))[None]
 
 
 def solution(mesh):

time: 222 us -> 187 us (0.84); the launches traced: 218 us -> 186 us
  Pallas kernels: 183 us -> 167 us
  matrix products: 12 us -> 1.87 us
  local copies, waits for them, and re-layouts: 8.53 us -> 3.3 us
    pallas_call x1, Pallas kernels: 86.7 us -> 70.6 us  [exchange(): pl.pallas_call(exchange_kernel, out_shape=jax.ShapeDtypeStruct(front.shap...]
    dot_general x2 -> x1, matrix products: 8.27 us -> 1.52 us  [contribution(): jnp.einsum('cq,cn->qn', column_table, spread.reshape(TILE_WIDTH, -1), pre...]
    unnamed x10 -> x7, local copies, waits for them, and re-layouts: 6.21 us -> 2.03 us
    dot_general x2 -> x1, matrix products: 3.73 us -> 0.35 us  [contribution(): spread = jnp.einsum('cei,eiq->ceq', shaped, row_table, precision=HIGHEST)]
  transfers between devices with their start and end apart: 2 -> 2, of which waited for: 1 -> 1; matrix products, arithmetic and copies ran while one was open for 0% -> 0% of each run, Pallas kernels for 65% -> 29%
where the time goes in v2:
time: 187 us; the launch traced here: 186 us
  Pallas kernels  167 us (89%)
  starting transfers between devices  9.67 us (5%)
  waiting for transfers between devices  3.53 us (2%)
  local copies, waits for them, and re-layouts  3.3 us (2%)
  matrix products  1.87 us (1%)
    pallas_call x1, Pallas kernels, exchange(): pl.pallas_call(exchange_kernel, out_shape=jax.ShapeDtypeStruct(front.shap...  70.6 us
    pallas_call x1, Pallas kernels, factor(): pl.pallas_call(factor_kernel, out_shape=jax.ShapeDtypeStruct((BLOCK, LEAD...  53.7 us
    pallas_call x1, Pallas kernels, share(): pl.pallas_call(share_kernel, out_shape=jax.ShapeDtypeStruct((LEAD_BLOCKS,...  42.8 us
    ppermute x2, starting transfers between devices, from_behind(): lax.ppermute(shard, 'blk', [(i, (i + by) % count) for i in range(count)])  9.67 us
  transfers between devices with their start and end apart: 2, of which 1 were waited for; matrix products, arithmetic and copies ran while one was open for 0% of the time, Pallas kernels for 29%

profile of v2, /device:TPU:8, one launch (start us, length us, event | category | flops | bytes accessed | tf_op | source)
XLA Modules:
  0.0 186.2 jit_solution(4695383331113606275)
XLA Ops:
  0.0 0.0 copy-start.2
  0.0 1.0 slice.26
  1.0 2.4 %collective-permute-start = (f32[64,512]{1,0:T(8,128)S(1)}, f32[64,512]{1,0:T(8,128)S(1)}, u32[]{:S(2)}, u32[]{:S(2)}) collective-permute-start(f32[64,512]{1,0:T(8,128)S(1)} %slice.26), channel_id=1, source_target_pairs={{0,32},{1,33},{2,34},{3,35},{4,36},{5,37},{6,38},{7,39},{8,40},{9,... | collective-permute-start | bytes 393224 | tf_op jit(solution)/shard_map/ppermute | solution.py:528
  3.4 0.7 add_select_fusion
  4.2 0.1 reshape.25
  4.2 0.1 slice.22
  4.3 3.5 %collective-permute-done = f32[64,512]{1,0:T(8,128)S(1)} collective-permute-done((f32[64,512]{1,0:T(8,128)S(1)}, f32[64,512]{1,0:T(8,128)S(1)}, u32[]{:S(2)}, u32[]{:S(2)}) %collective-permute-start) | collective-permute-done | bytes 131104 | tf_op jit(solution)/shard_map/ppermute | solution.py:528
  7.8 0.1 reshape.26
  7.9 0.3 convolution_bitcast_fusion
  8.3 1.5 convolution_add_fusion.own_ref
  9.8 0.0 copy-start
  9.8 0.0 copy-start.1
  9.9 42.8 %share.1.lead_ref = f32[8,128,1024]{2,1,0:T(8,128)S(1)} custom-call(f32[128,1024]{1,0:T(8,128)S(1)} %convolution_add_fusion.own_ref), custom_call_target="tpu_custom_call" | custom-call | tf_op jit(solution)/shard_map/share/pallas_call | solution.py:151
  52.6 0.0 copy-done.2
  52.6 7.3 %collective-permute-start.1 = (f32[64,4096]{1,0:T(8,128)S(1)}, f32[64,4096]{1,0:T(8,128)S(1)}, u32[]{:S(2)}, u32[]{:S(2)}) collective-permute-start(f32[64,4096]{1,0:T(8,128)S(1)} %bitcast.18), channel_id=1, source_target_pairs={{0,32},{1,33},{2,34},{3,35},{4,36},{5,37},{6,38},{7,39},{8,40},{9,... | collective-permute-start | bytes 3145736 | tf_op jit(solution)/shard_map/ppermute | solution.py:528
  59.9 53.7 %factor.1.l_ref = bf16[128,1024]{1,0:T(8,128)(2,1)S(1)} custom-call(s32[1]{0:T(128)} %bitcast.index_ref, f32[8,128,1024]{2,1,0:T(8,128)S(1)} %share.1.lead_ref, f32[128,1024]{1,0:T(8,128)S(1)} %convolution_add_fusion.own_ref), custom_call_target="tpu_custom_call" | custom-call | tf_op jit(solution)/shard_map/factor/pallas_call | solution.py:268
  113.6 0.0 collective-permute-done.1.tiles_ref
  113.6 0.0 copy-done
  113.6 0.0 copy-done.1
  113.6 70.6 %exchange.1 = f32[128,8192]{1,0:T(8,128)S(1)} custom-call(bf16[128,1024]{1,0:T(8,128)(2,1)S(1)} %factor.1.l_ref, f32[128,8192]{1,0:T(8,128)S(1)} %bitcast.15, f32[64,4096]{1,0:T(8,128)S(1)} %collective-permute-done.1.tiles_ref, s32[1,64]{1,0:T(1,128)S(1)} %constant_dynamic-slice_fusion.places_ref, s32[32,128]{1,0:T(8,128)S(1)} %bitcast.16), custom_call_target="tpu_custom_call" | custom-call | tf_op jit(solution)/shard_map/exchange/pallas_call | solution.py:496
  184.2 2.0 %copy.15 = f32[1,128,8192]{2,1,0:T(8,128)} copy(f32[1,128,8192]{2,1,0:T(8,128)S(1)} %bitcast.13) | data formatting | bytes 8388608
  (3 shorter events, 0.0 us)
Async XLA Ops:
  0.0 52.6 %copy-start.2 = (f32[1,64,4096]{2,1,0:T(8,128)S(1)}, f32[1,64,4096]{2,1,0:T(8,128)}, u32[]{:S(2)}) copy-start(f32[1,64,4096]{2,1,0:T(8,128)} %param.4) | copy-start | bytes 3145732
  1.0 6.8 %collective-permute-start = (f32[64,512]{1,0:T(8,128)S(1)}, f32[64,512]{1,0:T(8,128)S(1)}, u32[]{:S(2)}, u32[]{:S(2)}) collective-permute-start(f32[64,512]{1,0:T(8,128)S(1)} %slice.26), channel_id=1, source_target_pairs={{0,32},{1,33},{2,34},{3,35},{4,36},{5,37},{6,38},{7,39},{8,40},{9,... | collective-permute-start | bytes 393224 | tf_op jit(solution)/shard_map/ppermute | solution.py:528
  9.8 103.8 %copy-start = (f32[1,128,8192]{2,1,0:T(8,128)S(1)}, f32[1,128,8192]{2,1,0:T(8,128)}, u32[]{:S(2)}) copy-start(f32[1,128,8192]{2,1,0:T(8,128)} %param.3) | copy-start | bytes 12582916
  9.8 103.8 %copy-start.1 = (s32[4096]{0:T(1024)S(1)}, s32[4096]{0:T(1024)}, u32[]{:S(2)}) copy-start(s32[4096]{0:T(1024)} %param.5) | copy-start | bytes 49156
  52.6 61.0 %collective-permute-start.1 = (f32[64,4096]{1,0:T(8,128)S(1)}, f32[64,4096]{1,0:T(8,128)S(1)}, u32[]{:S(2)}, u32[]{:S(2)}) collective-permute-start(f32[64,4096]{1,0:T(8,128)S(1)} %bitcast.18), channel_id=1, source_target_pairs={{0,32},{1,33},{2,34},{3,35},{4,36},{5,37},{6,38},{7,39},{8,40},{9,... | collective-permute-start | bytes 3145736 | tf_op jit(solution)/shard_map/ppermute | solution.py:528

commit v3 on v2

--- a/solution.py
+++ b/solution.py
@@ -54,116 +54,6 @@
             barrier, inc=1, device_id=partner, device_id_type=pl.DeviceIdType.MESH
         )
     pl.semaphore_wait(barrier, len(partners))
-
-
-def pieces_of(s):
-    edges = [s * BLOCK] + [c for c in range(PIECE, LEAD + 1, PIECE) if c > s * BLOCK]
-    return list(zip(edges[:-1], edges[1:]))
-
-
-def share_kernel(own_ref, out_ref, local_sem, z_send, a_send, recv):
-    y, x, z = position()
-    greet(
-        [
-            device(1 - y, x, z),
-            device(y, x - 1, z),
-            device(y, x + 1, z),
-            device(y, x, z - 1),
-            device(y, x, z + 1),
-        ]
-    )
-    root = (y == 0) & (x == 0)
-
-    @pl.when(root)
-    def _():
-        copy = pltpu.make_async_copy(own_ref, out_ref.at[z], local_sem)
-        copy.start()
-        copy.wait()
-
-    def piece(s, p, send, target):
-        c0, c1 = pieces_of(s)[p]
-        part = out_ref.at[s, :, c0:c1]
-        return remote(part, part, send, recv.at[s, p], target)
-
-    def tree_sends(s, p):
-        onward = (x == 1) if p % 2 == 0 else (x == 3)
-        step = 1 if p % 2 == 0 else -1
-        return [
-            (root, piece(s, p, a_send.at[p, 0], device(1, x, z))),
-            (x == 0, piece(s, p, a_send.at[p, 1], device(y, x + 1, z))),
-            (x == 0, piece(s, p, a_send.at[p, 2], device(y, x - 1, z))),
-            (onward, piece(s, p, a_send.at[p, 3], device(y, x + step, z))),
-        ]
-
-    def up_hops(s):
-        return 4 if s % 2 == 0 else 3
-
-    def ring_sends(s, p, away):
-        ups = up_hops(s)
-        go_up = away < ups
-        go_down = (away == 0) | (away > ups + 1)
-        return [
-            (go_up, piece(s, p, z_send.at[s, p, 0], device(y, x, z + 1))),
-            (go_down, piece(s, p, z_send.at[s, p, 1], device(y, x, z - 1))),
-        ]
-
-    def start(sends):
-        for condition, copy in sends:
-            pl.when(condition)(copy.start)
-
-    def arrived(s, p):
-        piece(s, p, z_send.at[s, p, 0], device(y, x, z + 1)).wait_recv()
-
-    for s in range(LEAD_BLOCKS):
-
-        @pl.when(z == s)
-        def _(s=s):
-            for p in range(len(pieces_of(s))):
-                pl.when(jnp.logical_not(root))(lambda p=p: arrived(s, p))
-                start(tree_sends(s, p))
-                start(ring_sends(s, p, 0))
-
-    def hop(t, carry):
-        away = jnp.where(t % 2 == 1, (t + 1) // 2, Z - t // 2)
-        for s in range(LEAD_BLOCKS):
-
-            @pl.when(lax.rem(z - away + Z, Z) == s)
-            def _(s=s):
-                for p in range(len(pieces_of(s))):
-                    arrived(s, p)
-                    start(ring_sends(s, p, away))
-
-        return carry
-
-    lax.fori_loop(1, Z, hop, 0)
-
-    for s in range(LEAD_BLOCKS):
-        away = lax.rem(z - s + Z, Z)
-        for p in range(len(pieces_of(s))):
-            for condition, copy in ring_sends(s, p, away):
-                pl.when(condition)(copy.wait_send)
-            for condition, copy in tree_sends(s, p):
-                pl.when(condition & (away == 0))(copy.wait_send)
-
-
-def share(own):
-    most = LEAD // PIECE
-    return pl.pallas_call(
-        share_kernel,
-        out_shape=jax.ShapeDtypeStruct((LEAD_BLOCKS, BLOCK, LEAD), jnp.float32),
-        in_specs=[ANY],
-        out_specs=VMEM,
-        scratch_shapes=[
-            pltpu.SemaphoreType.DMA,
-            pltpu.SemaphoreType.DMA((LEAD_BLOCKS, most, 2)),
-            pltpu.SemaphoreType.DMA((most, 4)),
-            pltpu.SemaphoreType.DMA((LEAD_BLOCKS, most)),
-        ],
-        compiler_params=pltpu.CompilerParams(
-            collective_id=0, has_side_effects=True, vmem_limit_bytes=16 * MIB
-        ),
-        name="share",
-    )(own)
 
 
 def spread_out(x):
@@ -224,60 +114,216 @@
             x_ref[i : i + ROWS, :] = other
 
 
-def factor_kernel(index_ref, lead_ref, own_ref, l_ref, work, a_ref, x_ref):
-    width = LEAD + BLOCK
+PANEL_BLOCKS = PANEL_WIDTH // BLOCK
+WIDTH = PANEL_WIDTH + BLOCK
+
+
+def pieces_of(s, first):
+    edges = [s * BLOCK] + [c for c in range(PIECE, LEAD + 1, PIECE) if c > s * BLOCK]
+    spans = zip(edges[:-1], edges[1:])
+    return [((c1 - 1) // PIECE, c0, c1) for c0, c1 in spans if (c1 <= PANEL_WIDTH) == first]
+
+
+def factor_kernel(
+    own_ref, child_ref, l_ref, tiles_ref, lead, work, a_ref, x_ref, inverses,
+    local_sem, z_send, a_send, recv, tile_sem,
+):
+    y, x, z = position()
+    over = device(1 - y, x, z)
+    right, left = device(y, x + 1, z), device(y, x - 1, z)
+    up, down = device(y, x, z + 1), device(y, x, z - 1)
+    greet([over, right, left, up, down])
+    root = (y == 0) & (x == 0)
+
+    def piece(s, span, send, target):
+        p, c0, c1 = span
+        part = lead.at[s, :, c0:c1]
+        return remote(part, part, send, recv.at[s, p], target)
+
+    def tree_sends(s, span):
+        p = span[0]
+        onward = (x == 1) if p % 2 == 0 else (x == 3)
+        return [
+            (root, piece(s, span, a_send.at[p, 0], over)),
+            (x == 0, piece(s, span, a_send.at[p, 1], right)),
+            (x == 0, piece(s, span, a_send.at[p, 2], left)),
+            (onward, piece(s, span, a_send.at[p, 3], right if p % 2 == 0 else left)),
+        ]
+
+    def ring_sends(s, span, away):
+        p = span[0]
+        ups = Z // 2 if s % 2 == 0 else Z // 2 - 1
+        go_up = away < ups
+        go_down = (away == 0) | (away > ups + 1)
+        return [
+            (go_up, piece(s, span, z_send.at[s, p, 0], up)),
+            (go_down, piece(s, span, z_send.at[s, p, 1], down)),
+        ]
+
+    def start(sends):
+        for condition, copy in sends:
+            pl.when(condition)(copy.start)
+
+    def arrived(s, span):
+        piece(s, span, z_send.at[s, span[0], 0], up).wait_recv()
+
+    def each_slab(slab, first, act):
+        for s in range(LEAD_BLOCKS):
+            spans = pieces_of(s, first)
+            if spans:
+
+                @pl.when(slab == s)
+                def _(s=s, spans=spans):
+                    for span in spans:
+                        act(s, span)
+
+    def tree(first):
+        def act(s, span):
+            pl.when(jnp.logical_not(root))(lambda: arrived(s, span))
+            start(tree_sends(s, span))
+            if first:
+                start(ring_sends(s, span, 0))
+
+        each_slab(z, first, act)
+
+    def hop(t, first):
+        away = jnp.where(lax.rem(t, 2) == 1, (t + 1) // 2, Z - t // 2)
+
+        def act(s, span):
+            arrived(s, span)
+            start(ring_sends(s, span, away))
+
+        each_slab(lax.rem(z - away + Z, Z), first, act)
+
+    @pl.when(root)
+    def _():
+        copy = pltpu.make_async_copy(own_ref, lead.at[z], local_sem)
+        copy.start()
+        copy.wait()
+
+    tree(True)
+    level = y + jnp.where(x == 0, 0, 1) + jnp.where(x == 2, 1, 0)
+    turn = jnp.where(level == 0, 1, jnp.where(level == 1, 3, jnp.where(level == 2, 6, 8)))
     for s in range(LEAD_BLOCKS):
-        work[s, :, 0:LEAD] = lead_ref[s]
-        work[s, :, LEAD:width] = own_ref[:, s * BLOCK : (s + 1) * BLOCK].T
-    per_panel = PANEL_WIDTH // BLOCK
+        own_part = own_ref[:, s * BLOCK : (s + 1) * BLOCK].T
+        work[s, :, PANEL_WIDTH:WIDTH] = own_part
+
+    def first_hops(t, carry):
+        pl.when(t == turn)(lambda: tree(False))
+        pl.when(t < Z)(lambda: hop(t, True))
+        return carry
+
+    lax.fori_loop(1, Z + 1, first_hops, 0)
+    each_slab(z, False, lambda s, span: start(ring_sends(s, span, 0)))
+    for s in range(PANEL_BLOCKS):
+        work[s, :, 0:PANEL_WIDTH] = lead[s, :, 0:PANEL_WIDTH]
+
+    tiles_copy = remote(child_ref, tiles_ref, tile_sem.at[0], tile_sem.at[1], over)
 
     def step(b, carry):
-        a_ref[...] = work[b, :, pl.ds(pl.multiple_of(b * BLOCK, BLOCK), BLOCK)]
+        panel = b // PANEL_BLOCKS
+        window = pl.ds(pl.multiple_of(panel * PANEL_WIDTH, BLOCK), WIDTH)
+
+        def block(t):
+            return pl.ds(pl.multiple_of((t + panel) * BLOCK, BLOCK), BLOCK)
+
+        @pl.when((b > 0) & (b < PANEL_BLOCKS))
+        def _():
+            def act(t, carry):
+                hop(t, False)
+                return carry
+
+            lax.fori_loop(2 * b - 1, 2 * b + 1, act, 0)
+
+        pl.when(b == PANEL_BLOCKS)(tiles_copy.start)
+        a_ref[...] = work[b, :, block(b)]
         invert_factor(a_ref, x_ref)
-        work[b] = dot(x_ref[...], work[b])
+        inverses[b] = x_ref[...]
+        work[b, :, window] = dot(x_ref[...], work[b, :, window])
 
         def update(t, carry):
-            crossing = work[b, :, pl.ds(pl.multiple_of(t * BLOCK, BLOCK), BLOCK)]
-            work[t] = work[t] - dot(crossing, work[b], ((0,), (0,)))
+            crossing = work[b, :, block(t)]
+            work[t, :, window] = work[t, :, window] - dot(crossing, work[b, :, window], ((0,), (0,)))
             return carry
 
-        lax.fori_loop(b + 1, (b // per_panel + 1) * per_panel, update, 0)
-
-        @pl.when(b == per_panel - 1)
+        lax.fori_loop(b + 1, (panel + 1) * PANEL_BLOCKS, update, 0)
+
+        @pl.when(b == PANEL_BLOCKS - 1)
         def _():
-            first = work[0:per_panel, :, PANEL_WIDTH:width].astype(jnp.bfloat16)
-            first = first.reshape(PANEL_WIDTH, width - PANEL_WIDTH)
-            for t in range(per_panel):
-                rows = work[per_panel + t, :, PANEL_WIDTH:width]
-                crossing = first[:, t * BLOCK : (t + 1) * BLOCK]
-                work[per_panel + t, :, PANEL_WIDTH:width] = rows - dot(
+            hop(jnp.full((), Z - 1, jnp.int32), False)
+            for s in range(LEAD_BLOCKS):
+                work[s, :, WIDTH:] = lead[s, :, PANEL_WIDTH:LEAD]
+
+            def solve(s, carry):
+                work[s, :, WIDTH:] = dot(inverses[s], work[s, :, WIDTH:])
+
+                def update(t, carry):
+                    crossing = work[s, :, pl.ds(pl.multiple_of(t * BLOCK, BLOCK), BLOCK)]
+                    rest = dot(crossing, work[s, :, WIDTH:], ((0,), (0,)))
+                    work[t, :, WIDTH:] = work[t, :, WIDTH:] - rest
+                    return carry
+
+                lax.fori_loop(s + 1, PANEL_BLOCKS, update, 0)
+                return carry
+
+            lax.fori_loop(0, PANEL_BLOCKS, solve, 0)
+            first = work[0:PANEL_BLOCKS, :, PANEL_WIDTH:].astype(jnp.bfloat16)
+            first = first.reshape(PANEL_WIDTH, WIDTH)
+            for t in range(PANEL_BLOCKS):
+                rows = work[PANEL_BLOCKS + t, :, PANEL_WIDTH:]
+                crossing = first[:, (t + 1) * BLOCK : (t + 2) * BLOCK]
+                work[PANEL_BLOCKS + t, :, PANEL_WIDTH:] = rows - dot(
                     crossing, first, ((0,), (0,)), None
                 )
 
         return carry
 
     lax.fori_loop(0, LEAD_BLOCKS, step, 0)
+    mine = ((y * X + x) * Z + z) * BLOCK
     for s in range(LEAD_BLOCKS):
         q = lax.broadcasted_iota(jnp.int32, (BLOCK, BLOCK), 0) + s * BLOCK
-        c = lax.broadcasted_iota(jnp.int32, (BLOCK, BLOCK), 1) + index_ref[0] * BLOCK
-        own = jnp.where(q <= c, work[s, :, LEAD:width], 0.0)
+        c = lax.broadcasted_iota(jnp.int32, (BLOCK, BLOCK), 1) + mine
+        own = jnp.where(q <= c, work[s, :, PANEL_WIDTH:WIDTH], 0.0)
         l_ref[:, s * BLOCK : (s + 1) * BLOCK] = own.T.astype(jnp.bfloat16)
 
-
-def factor(index, lead, own):
+    tiles_copy.wait()
+    for s in range(LEAD_BLOCKS):
+        away = lax.rem(z - s + Z, Z)
+        for span in pieces_of(s, True) + pieces_of(s, False):
+            for condition, copy in ring_sends(s, span, away):
+                pl.when(condition)(copy.wait_send)
+            for condition, copy in tree_sends(s, span):
+                pl.when(condition & (away == 0))(copy.wait_send)
+
+
+def factor(own, child):
+    dma = pltpu.SemaphoreType.DMA
+    f32 = jnp.float32
     return pl.pallas_call(
         factor_kernel,
-        out_shape=jax.ShapeDtypeStruct((BLOCK, LEAD), jnp.bfloat16),
-        in_specs=[pl.BlockSpec(memory_space=pltpu.SMEM), VMEM, VMEM],
-        out_specs=VMEM,
+        out_shape=[
+            jax.ShapeDtypeStruct((BLOCK, LEAD), jnp.bfloat16),
+            jax.ShapeDtypeStruct(child.shape, f32),
+        ],
+        in_specs=[VMEM, ANY],
+        out_specs=[VMEM, VMEM],
         scratch_shapes=[
-            pltpu.VMEM((LEAD_BLOCKS, BLOCK, LEAD + BLOCK), jnp.float32),
-            pltpu.VMEM((BLOCK, BLOCK), jnp.float32),
-            pltpu.VMEM((BLOCK, BLOCK), jnp.float32),
+            pltpu.VMEM((LEAD_BLOCKS, BLOCK, LEAD), f32),
+            pltpu.VMEM((LEAD_BLOCKS, BLOCK, LEAD + BLOCK), f32),
+            pltpu.VMEM((BLOCK, BLOCK), f32),
+            pltpu.VMEM((BLOCK, BLOCK), f32),
+            pltpu.VMEM((LEAD_BLOCKS, BLOCK, BLOCK), f32),
+            dma,
+            dma((LEAD_BLOCKS, LEAD // PIECE, 2)),
+            dma((LEAD // PIECE, 4)),
+            dma((LEAD_BLOCKS, LEAD // PIECE)),
+            dma((2,)),
         ],
-        compiler_params=pltpu.CompilerParams(vmem_limit_bytes=32 * MIB),
+        compiler_params=pltpu.CompilerParams(
+            collective_id=0, has_side_effects=True, vmem_limit_bytes=32 * MIB
+        ),
         name="factor",
-    )(index, lead, own)
+    )(own, child)
 
 
 STEPS = 2 * X
@@ -551,10 +597,7 @@
     own = front[:, :LEAD] + contribution(
         early_tiles, places[half : half + LEAD_BLOCKS], own_places
     )
-    lead = share(own)
-    lead, child = lax.optimization_barrier((lead, child))
-    tiles = from_behind(child, half)
-    rows = factor(index[None].astype(jnp.int32), lead, own)
+    rows, tiles = factor(own, child)
     return exchange(rows, front, tiles, own_places[None], index_map.reshape(-1, BLOCK))[None]
 
 

time: 187 us -> 171 us (0.914)
  the two profiles are of different devices: /device:TPU:8 before, /device:TPU:12 now
where the time goes in v3:
time: 171 us
  Pallas kernels  156 us (91%)
  local copies, waits for them, and re-layouts  6.62 us (4%)
  waiting for transfers between devices  3.55 us (2%)
  starting transfers between devices  2.38 us (1%)
  matrix products  1.87 us (1%)
    pallas_call x1, Pallas kernels, factor(): pl.pallas_call(factor_kernel, out_shape=[jax.ShapeDtypeStruct((BLOCK, LEA...  88.9 us
    pallas_call x1, Pallas kernels, exchange(): pl.pallas_call(exchange_kernel, out_shape=jax.ShapeDtypeStruct(front.shap...  67.1 us
    unnamed x7, local copies, waits for them, and re-layouts  5.42 us
    ppermute x1, waiting for transfers between devices, from_behind(): lax.ppermute(shard, 'blk', [(i, (i + by) % count) for i in range(count)])  3.55 us
  transfers between devices with their start and end apart: 1, of which 1 were waited for; matrix products, arithmetic and copies ran while one was open for 1% of the time, Pallas kernels for 0%

profile of v3, /device:TPU:12, one launch (start us, length us, event | category | flops | bytes accessed | tf_op | source)
XLA Modules:
  0.0 171.2 jit_solution(1929886829274064882)
XLA Ops:
  0.0 0.0 copy-start.2
  0.0 0.9 slice.26
  0.9 2.4 %collective-permute-start = (f32[64,512]{1,0:T(8,128)S(1)}, f32[64,512]{1,0:T(8,128)S(1)}, u32[]{:S(2)}, u32[]{:S(2)}) collective-permute-start(f32[64,512]{1,0:T(8,128)S(1)} %slice.26), channel_id=1, source_target_pairs={{0,32},{1,33},{2,34},{3,35},{4,36},{5,37},{6,38},{7,39},{8,40},{9,... | collective-permute-start | bytes 393224 | tf_op jit(solution)/shard_map/ppermute | solution.py:574
  3.3 0.7 add_select_fusion
  4.0 0.1 reshape.25
  4.1 0.1 slice.22
  4.2 3.5 %collective-permute-done = f32[64,512]{1,0:T(8,128)S(1)} collective-permute-done((f32[64,512]{1,0:T(8,128)S(1)}, f32[64,512]{1,0:T(8,128)S(1)}, u32[]{:S(2)}, u32[]{:S(2)}) %collective-permute-start) | collective-permute-done | bytes 131104 | tf_op jit(solution)/shard_map/ppermute | solution.py:574
  7.8 0.1 reshape.26
  7.9 0.3 convolution_bitcast_fusion
  8.2 1.5 convolution_add_fusion.own_ref
  9.7 0.0 copy-start.1
  9.8 1.2 copy-done.1
  11.0 88.9 %factor.1 = (bf16[128,1024]{1,0:T(8,128)(2,1)S(1)}, f32[64,4096]{1,0:T(8,128)S(1)}) custom-call(f32[128,1024]{1,0:T(8,128)S(1)} %convolution_add_fusion.own_ref, f32[64,4096]{1,0:T(8,128)S(1)} %bitcast.16), custom_call_target="tpu_custom_call" | custom-call | tf_op jit(solution)/shard_map/factor/pallas_call | solution.py:302
  99.9 0.0 copy-done.2
  99.9 0.0 copy-start
  99.9 2.2 %copy-done = f32[1,128,8192]{2,1,0:T(8,128)S(1)} copy-done((f32[1,128,8192]{2,1,0:T(8,128)S(1)}, f32[1,128,8192]{2,1,0:T(8,128)}, u32[]{:S(2)}) %copy-start) | copy-done | bytes 4194328
  102.1 67.1 %exchange.1 = f32[128,8192]{1,0:T(8,128)S(1)} custom-call(bf16[128,1024]{1,0:T(8,128)(2,1)S(1)} %get-tuple-element.7.l_ref, f32[128,8192]{1,0:T(8,128)S(1)} %bitcast.14, f32[64,4096]{1,0:T(8,128)S(1)} %get-tuple-element.8.tiles_ref, s32[1,64]{1,0:T(1,128)S(1)} %constant_dynamic-slice_fusion.places_ref, s32[32,128]{1,0:T(8,128)S(1)} %bitcast.17), custom_call_target="tpu_custom_call" | custom-call | tf_op jit(solution)/shard_map/exchange/pallas_call | solution.py:542
  169.2 2.0 %copy.15 = f32[1,128,8192]{2,1,0:T(8,128)} copy(f32[1,128,8192]{2,1,0:T(8,128)S(1)} %bitcast.12) | data formatting | bytes 8388608
  (3 shorter events, 0.0 us)
Async XLA Ops:
  0.0 99.9 %copy-start.2 = (s32[4096]{0:T(1024)S(1)}, s32[4096]{0:T(1024)}, u32[]{:S(2)}) copy-start(s32[4096]{0:T(1024)} %param.5) | copy-start | bytes 49156
  0.9 6.8 %collective-permute-start = (f32[64,512]{1,0:T(8,128)S(1)}, f32[64,512]{1,0:T(8,128)S(1)}, u32[]{:S(2)}, u32[]{:S(2)}) collective-permute-start(f32[64,512]{1,0:T(8,128)S(1)} %slice.26), channel_id=1, source_target_pairs={{0,32},{1,33},{2,34},{3,35},{4,36},{5,37},{6,38},{7,39},{8,40},{9,... | collective-permute-start | bytes 393224 | tf_op jit(solution)/shard_map/ppermute | solution.py:574
  9.7 1.2 copy-start.1
  99.9 2.2 %copy-start = (f32[1,128,8192]{2,1,0:T(8,128)S(1)}, f32[1,128,8192]{2,1,0:T(8,128)}, u32[]{:S(2)}) copy-start(f32[1,128,8192]{2,1,0:T(8,128)} %param.3) | copy-start | bytes 12582916

commit v4 on v3

--- a/solution.py
+++ b/solution.py
@@ -13,11 +13,11 @@
 ROWS = 8
 Z = 8
 X = 4
-PIECE = 256
+PIECE = 128
 
 HIGHEST = lax.Precision.HIGHEST
-ANY = pl.BlockSpec(memory_space=pl.ANY)
 VMEM = pl.BlockSpec(memory_space=pltpu.VMEM)
+HBM = pl.BlockSpec(memory_space=pltpu.HBM)
 MIB = 1024 * 1024
 
 
@@ -60,11 +60,6 @@
     return jnp.broadcast_to(x, (ROWS, BLOCK))
 
 
-def refined_rsqrt(d):
-    guess = lax.rsqrt(d)
-    return guess * (1.5 - 0.5 * d * guess * guess)
-
-
 def eliminate(parts, low, inv):
     done = []
     for r in range(ROWS):
@@ -80,7 +75,7 @@
     low = [[None] * ROWS for _ in range(ROWS)]
     inv = [None] * ROWS
     for s in range(ROWS):
-        inv[s] = refined_rsqrt(a[s][s])
+        inv[s] = lax.rsqrt(a[s][s])
         for r in range(s + 1, ROWS):
             low[r][s] = a[r][s] * inv[s]
         for r in range(s + 1, ROWS):
@@ -124,21 +119,134 @@
     return [((c1 - 1) // PIECE, c0, c1) for c0, c1 in spans if (c1 <= PANEL_WIDTH) == first]
 
 
-def factor_kernel(
-    own_ref, child_ref, l_ref, tiles_ref, lead, work, a_ref, x_ref, inverses,
-    local_sem, z_send, a_send, recv, tile_sem,
+STEPS = 2 * X
+
+
+def front_kernel(
+    own_ref, child_ref, front_ref, places_ref, index_ref, out_ref,
+    lead, work, a_ref, x_ref, inverses, tiles, staged,
+    line, plane, made, came, z_made, z_came, picked,
+    local_sem, b_send, a_send, b_recv, tile_sem, own_sem,
+    l_send, l_recv, p_send, p_recv, q_send, q_recv, z_send, z_recv,
 ):
     y, x, z = position()
+    a = y * X + x
     over = device(1 - y, x, z)
     right, left = device(y, x + 1, z), device(y, x - 1, z)
     up, down = device(y, x, z + 1), device(y, x, z - 1)
-    greet([over, right, left, up, down])
-    root = (y == 0) & (x == 0)
+
+    def plane_index(slot):
+        return lax.rem(y + slot // X, 2) * X + lax.rem(x + lax.rem(slot, X), X)
+
+    def plane_device(slot):
+        return {"blk": plane_index(slot) * Z + z}
+
+    greet([up, down] + [plane_device(slot) for slot in range(1, STEPS)])
+    base = pltpu.make_async_copy(front_ref, out_ref, local_sem.at[1])
+    base.start()
+    root = a == 0
+
+    def rows(slot, half=None):
+        if half is None:
+            return pl.ds(slot * BLOCK, BLOCK)
+        return pl.ds(slot * BLOCK + half * (BLOCK // 2), BLOCK // 2)
+
+    def panel_columns(panel):
+        return pl.ds(panel * PANEL_WIDTH, PANEL_WIDTH)
+
+    def own_copies(panel):
+        return [
+            pltpu.make_async_copy(
+                staged.at[panel], target.at[rows(0), panel_columns(panel)], own_sem.at[panel, i]
+            )
+            for i, target in enumerate((line, plane))
+        ]
+
+    def keep_rows(panel):
+        for i in range(PANEL_BLOCKS):
+            s = panel * PANEL_BLOCKS + i
+            q = lax.broadcasted_iota(jnp.int32, (BLOCK, BLOCK), 0) + s * BLOCK
+            c = lax.broadcasted_iota(jnp.int32, (BLOCK, BLOCK), 1) + (a * Z + z) * BLOCK
+            own = jnp.where(q <= c, work[s, :, PANEL_WIDTH:WIDTH], 0.0)
+            staged[panel, :, i * BLOCK : (i + 1) * BLOCK] = own.T.astype(jnp.bfloat16)
+        for copy in own_copies(panel):
+            copy.start()
+
+    def line_copy(panel, way, hop):
+        half = None if hop < Z // 2 else way
+        sign = -1 if way == 0 else 1
+        start, end = (sign * (hop - 1)) % Z, (sign * hop) % Z
+        return remote(
+            line.at[rows(start, half), panel_columns(panel)],
+            line.at[rows(end, half), panel_columns(panel)],
+            l_send.at[panel, way, hop - 1],
+            l_recv.at[panel, way, hop - 1],
+            up if way == 0 else down,
+        )
+
+    def across(panel, number):
+        start, end, half, target = [
+            (0, 4, None, over),
+            (0, 3, None, right),
+            (0, 1, None, left),
+            (4, 7, None, right),
+            (4, 5, None, left),
+            (3, 2, 0, right),
+            (1, 2, 1, left),
+            (7, 6, 0, right),
+            (5, 6, 1, left),
+        ][number]
+        return remote(
+            plane.at[rows(start, half), panel_columns(panel)],
+            plane.at[rows(end, half), panel_columns(panel)],
+            p_send.at[panel, number],
+            p_recv.at[panel, number],
+            target,
+        )
+
+    def gather(panel):
+        along, beside = own_copies(panel)
+        along.wait()
+        line_copy(panel, 0, 1).start()
+        line_copy(panel, 1, 1).start()
+        beside.wait()
+        for number in (0, 1, 2):
+            across(panel, number).start()
+
+    def pass_on(panel, hop):
+        for way in (0, 1):
+            line_copy(panel, way, hop).wait_recv()
+            line_copy(panel, way, hop + 1).start()
+
+    def pass_across(panel, number, *onward):
+        across(panel, number).wait_recv()
+        for other in onward:
+            across(panel, other).start()
+
+    def gather_first(panel):
+        pass_on(panel, 1)
+        pass_across(panel, 0, 3, 4)
+        pass_across(panel, 1, 5)
+        pass_across(panel, 2, 6)
+
+    def gather_second(panel):
+        pass_on(panel, 2)
+        pass_across(panel, 3, 7)
+        pass_across(panel, 4, 8)
+
+    def gather_third(panel):
+        pass_on(panel, 3)
+
+    def gather_last(panel):
+        for number in (5, 6, 7, 8):
+            across(panel, number).wait_recv()
+        for way in (0, 1):
+            line_copy(panel, way, Z // 2).wait_recv()
 
     def piece(s, span, send, target):
         p, c0, c1 = span
         part = lead.at[s, :, c0:c1]
-        return remote(part, part, send, recv.at[s, p], target)
+        return remote(part, part, send, b_recv.at[s, p], target)
 
     def tree_sends(s, span):
         p = span[0]
@@ -156,8 +264,8 @@
         go_up = away < ups
         go_down = (away == 0) | (away > ups + 1)
         return [
-            (go_up, piece(s, span, z_send.at[s, p, 0], up)),
-            (go_down, piece(s, span, z_send.at[s, p, 1], down)),
+            (go_up, piece(s, span, b_send.at[s, p, 0], up)),
+            (go_down, piece(s, span, b_send.at[s, p, 1], down)),
         ]
 
     def start(sends):
@@ -165,7 +273,7 @@
             pl.when(condition)(copy.start)
 
     def arrived(s, span):
-        piece(s, span, z_send.at[s, span[0], 0], up).wait_recv()
+        piece(s, span, b_send.at[s, span[0], 0], up).wait_recv()
 
     def each_slab(slab, first, act):
         for s in range(LEAD_BLOCKS):
@@ -197,7 +305,7 @@
 
     @pl.when(root)
     def _():
-        copy = pltpu.make_async_copy(own_ref, lead.at[z], local_sem)
+        copy = pltpu.make_async_copy(own_ref, lead.at[z], local_sem.at[0])
         copy.start()
         copy.wait()
 
@@ -218,7 +326,7 @@
     for s in range(PANEL_BLOCKS):
         work[s, :, 0:PANEL_WIDTH] = lead[s, :, 0:PANEL_WIDTH]
 
-    tiles_copy = remote(child_ref, tiles_ref, tile_sem.at[0], tile_sem.at[1], over)
+    tiles_copy = remote(child_ref, tiles, tile_sem.at[0], tile_sem.at[1], over)
 
     def step(b, carry):
         panel = b // PANEL_BLOCKS
@@ -235,10 +343,14 @@
 
             lax.fori_loop(2 * b - 1, 2 * b + 1, act, 0)
 
-        pl.when(b == PANEL_BLOCKS)(tiles_copy.start)
+        pl.when(b == 2)(tiles_copy.start)
+        pl.when(b == PANEL_BLOCKS + 1)(lambda: gather_first(0))
+        pl.when(b == PANEL_BLOCKS + 2)(lambda: gather_third(0))
         a_ref[...] = work[b, :, block(b)]
         invert_factor(a_ref, x_ref)
         inverses[b] = x_ref[...]
+        pl.when(b == PANEL_BLOCKS)(lambda: gather(0))
+        pl.when(b == PANEL_BLOCKS + 1)(lambda: gather_second(0))
         work[b, :, window] = dot(x_ref[...], work[b, :, window])
 
         def update(t, carry):
@@ -275,134 +387,20 @@
                 work[PANEL_BLOCKS + t, :, PANEL_WIDTH:] = rows - dot(
                     crossing, first, ((0,), (0,)), None
                 )
+            keep_rows(0)
 
         return carry
 
     lax.fori_loop(0, LEAD_BLOCKS, step, 0)
-    mine = ((y * X + x) * Z + z) * BLOCK
-    for s in range(LEAD_BLOCKS):
-        q = lax.broadcasted_iota(jnp.int32, (BLOCK, BLOCK), 0) + s * BLOCK
-        c = lax.broadcasted_iota(jnp.int32, (BLOCK, BLOCK), 1) + mine
-        own = jnp.where(q <= c, work[s, :, PANEL_WIDTH:WIDTH], 0.0)
-        l_ref[:, s * BLOCK : (s + 1) * BLOCK] = own.T.astype(jnp.bfloat16)
-
-    tiles_copy.wait()
-    for s in range(LEAD_BLOCKS):
-        away = lax.rem(z - s + Z, Z)
-        for span in pieces_of(s, True) + pieces_of(s, False):
-            for condition, copy in ring_sends(s, span, away):
-                pl.when(condition)(copy.wait_send)
-            for condition, copy in tree_sends(s, span):
-                pl.when(condition & (away == 0))(copy.wait_send)
-
-
-def factor(own, child):
-    dma = pltpu.SemaphoreType.DMA
-    f32 = jnp.float32
-    return pl.pallas_call(
-        factor_kernel,
-        out_shape=[
-            jax.ShapeDtypeStruct((BLOCK, LEAD), jnp.bfloat16),
-            jax.ShapeDtypeStruct(child.shape, f32),
-        ],
-        in_specs=[VMEM, ANY],
-        out_specs=[VMEM, VMEM],
-        scratch_shapes=[
-            pltpu.VMEM((LEAD_BLOCKS, BLOCK, LEAD), f32),
-            pltpu.VMEM((LEAD_BLOCKS, BLOCK, LEAD + BLOCK), f32),
-            pltpu.VMEM((BLOCK, BLOCK), f32),
-            pltpu.VMEM((BLOCK, BLOCK), f32),
-            pltpu.VMEM((LEAD_BLOCKS, BLOCK, BLOCK), f32),
-            dma,
-            dma((LEAD_BLOCKS, LEAD // PIECE, 2)),
-            dma((LEAD // PIECE, 4)),
-            dma((LEAD_BLOCKS, LEAD // PIECE)),
-            dma((2,)),
-        ],
-        compiler_params=pltpu.CompilerParams(
-            collective_id=0, has_side_effects=True, vmem_limit_bytes=32 * MIB
-        ),
-        name="factor",
-    )(own, child)
-
-
-STEPS = 2 * X
-
-
-def exchange_kernel(
-    l_ref, front_ref, tiles_ref, places_ref, index_ref, out_ref,
-    line, plane, made, came, z_made, z_came, picked,
-    local_sem, l_send, l_recv, p_send, p_recv, q_send, q_recv, z_send, z_recv,
-):
-    y, x, z = position()
-    a = y * X + x
-    up, down = device(y, x, z + 1), device(y, x, z - 1)
-    right, left, over = device(y, x + 1, z), device(y, x - 1, z), device(1 - y, x, z)
-
-    def plane_index(slot):
-        return lax.rem(y + slot // X, 2) * X + lax.rem(x + lax.rem(slot, X), X)
-
-    def plane_device(slot):
-        return {"blk": plane_index(slot) * Z + z}
-
-    greet([up, down] + [plane_device(slot) for slot in range(1, STEPS)])
-
-    def rows(slot, half=None):
-        if half is None:
-            return pl.ds(slot * BLOCK, BLOCK)
-        return pl.ds(slot * BLOCK + half * (BLOCK // 2), BLOCK // 2)
-
-    own_line = pltpu.make_async_copy(l_ref, line.at[rows(0)], local_sem.at[0])
-    own_plane = pltpu.make_async_copy(l_ref, plane.at[rows(0)], local_sem.at[1])
-    base = pltpu.make_async_copy(front_ref, out_ref, local_sem.at[2])
-    own_line.start()
-    own_plane.start()
-    base.start()
-
-    def line_copy(way, hop):
-        half = None if hop < Z // 2 else way
-        sign = -1 if way == 0 else 1
-        start, end = (sign * (hop - 1)) % Z, (sign * hop) % Z
-        return remote(
-            line.at[rows(start, half)],
-            line.at[rows(end, half)],
-            l_send.at[way, hop - 1],
-            l_recv.at[way, hop - 1],
-            up if way == 0 else down,
-        )
-
-    def plane_copy(number, start, end, half, target):
-        return remote(
-            plane.at[rows(start, half)],
-            plane.at[rows(end, half)],
-            p_send.at[number],
-            p_recv.at[number],
-            target,
-        )
-
-    across = [
-        plane_copy(0, 0, 4, None, over),
-        plane_copy(1, 0, 3, None, right),
-        plane_copy(2, 0, 1, None, left),
-        plane_copy(3, 4, 7, None, right),
-        plane_copy(4, 4, 5, None, left),
-        plane_copy(5, 3, 2, 0, right),
-        plane_copy(6, 1, 2, 1, left),
-        plane_copy(7, 7, 6, 0, right),
-        plane_copy(8, 5, 6, 1, left),
-    ]
-    own_line.wait()
-    line_copy(0, 1).start()
-    line_copy(1, 1).start()
-    own_plane.wait()
-    for number in (0, 1, 2):
-        across[number].start()
+    keep_rows(1)
+    gather(1)
+    tiles_copy.wait_recv()
 
     slot_of = lax.broadcasted_iota(jnp.int32, (BLOCK, TILE_WIDTH), 0)
     column_table = jnp.where(slot_of == places_ref[...], 1.0, 0.0).astype(jnp.float32)
     order = picked.shape[1]
     for start in range(0, order, LEAD):
-        picked[:, start : start + LEAD] = dot(column_table, tiles_ref[:, start : start + LEAD])
+        picked[:, start : start + LEAD] = dot(column_table, tiles[:, start : start + LEAD])
     pairs = order // BLOCK
 
     def place(pair, carry):
@@ -414,32 +412,15 @@
         out_ref[:, columns] = out_ref[:, columns] + dot(part, row_table, ((1,), (1,)))
         return carry
 
-    def pass_on(hop):
-        for way in (0, 1):
-            line_copy(way, hop).wait_recv()
-            line_copy(way, hop + 1).start()
-
-    def pass_across(number, *onward):
-        across[number].wait_recv()
-        for other in onward:
-            across[other].start()
-
-    pass_on(1)
-    pass_across(0, 3, 4)
-    pass_across(1, 5)
-    pass_across(2, 6)
+    gather_first(1)
     base.wait()
     lax.fori_loop(0, pairs // 4, place, 0)
-    pass_on(2)
-    pass_across(3, 7)
-    pass_across(4, 8)
+    gather_second(1)
     lax.fori_loop(pairs // 4, pairs // 2, place, 0)
-    pass_on(3)
+    gather_third(1)
     lax.fori_loop(pairs // 2, pairs, place, 0)
-    for number in (5, 6, 7, 8):
-        pass_across(number)
-    for way in (0, 1):
-        line_copy(way, Z // 2).wait_recv()
+    gather_last(0)
+    gather_last(1)
 
     def lefts(block, holder, zz):
         j = lax.broadcasted_iota(jnp.int32, (BLOCK, LEAD), 0) + lax.rem(zz + Z, Z) * BLOCK
@@ -530,43 +511,65 @@
         pl.when(sends)(product_copy(slot).wait_send)
     for way in (0, 1):
         z_copy(way).wait_send()
-        for hop in range(1, Z // 2 + 1):
-            line_copy(way, hop).wait_send()
-    for copy in across:
-        copy.wait_send()
-
-
-def exchange(rows, front, tiles, places, index_map):
+    tiles_copy.wait_send()
+    for panel in (0, 1):
+        for way in (0, 1):
+            for hop_number in range(1, Z // 2 + 1):
+                line_copy(panel, way, hop_number).wait_send()
+        for number in range(9):
+            across(panel, number).wait_send()
+    for s in range(LEAD_BLOCKS):
+        away = lax.rem(z - s + Z, Z)
+        for span in pieces_of(s, True) + pieces_of(s, False):
+            for condition, copy in ring_sends(s, span, away):
+                pl.when(condition)(copy.wait_send)
+            for condition, copy in tree_sends(s, span):
+                pl.when(condition & (away == 0))(copy.wait_send)
+
+
+def whole(own, child, front, places, index_map):
     dma = pltpu.SemaphoreType.DMA
-    f32 = jnp.float32
+    f32, bf16 = jnp.float32, jnp.bfloat16
     return pl.pallas_call(
-        exchange_kernel,
+        front_kernel,
         out_shape=jax.ShapeDtypeStruct(front.shape, f32),
-        in_specs=[ANY, ANY, VMEM, VMEM, VMEM],
+        in_specs=[VMEM, HBM, HBM, VMEM, VMEM],
         out_specs=VMEM,
         scratch_shapes=[
-            pltpu.VMEM((Z * BLOCK, LEAD), jnp.bfloat16),
-            pltpu.VMEM((STEPS * BLOCK, LEAD), jnp.bfloat16),
+            pltpu.VMEM((LEAD_BLOCKS, BLOCK, LEAD), f32),
+            pltpu.VMEM((LEAD_BLOCKS, BLOCK, LEAD + BLOCK), f32),
+            pltpu.VMEM((BLOCK, BLOCK), f32),
+            pltpu.VMEM((BLOCK, BLOCK), f32),
+            pltpu.VMEM((LEAD_BLOCKS, BLOCK, BLOCK), f32),
+            pltpu.VMEM(child.shape, f32),
+            pltpu.VMEM((2, BLOCK, PANEL_WIDTH), bf16),
+            pltpu.VMEM((Z * BLOCK, LEAD), bf16),
+            pltpu.VMEM((STEPS * BLOCK, LEAD), bf16),
             pltpu.VMEM((STEPS, BLOCK, 5 * BLOCK), f32),
             pltpu.VMEM((STEPS, BLOCK, 5 * BLOCK), f32),
             pltpu.VMEM((2, BLOCK, 7 * BLOCK), f32),
             pltpu.VMEM((2, BLOCK, 7 * BLOCK), f32),
-            pltpu.VMEM((BLOCK, tiles.shape[1]), f32),
-            dma((3,)),
-            dma((2, Z // 2)),
-            dma((2, Z // 2)),
-            dma((9,)),
-            dma((9,)),
+            pltpu.VMEM((BLOCK, child.shape[1]), f32),
+            dma((2,)),
+            dma((LEAD_BLOCKS, LEAD // PIECE, 2)),
+            dma((LEAD // PIECE, 4)),
+            dma((LEAD_BLOCKS, LEAD // PIECE)),
+            dma((2,)),
+            dma((2, 2)),
+            dma((2, 2, Z // 2)),
+            dma((2, 2, Z // 2)),
+            dma((2, 9)),
+            dma((2, 9)),
             dma((STEPS,)),
             dma((STEPS,)),
             dma((2,)),
             dma((2,)),
         ],
         compiler_params=pltpu.CompilerParams(
-            collective_id=1, has_side_effects=True, vmem_limit_bytes=40 * MIB
+            collective_id=0, has_side_effects=True, vmem_limit_bytes=48 * MIB
         ),
-        name="exchange",
-    )(rows, front, tiles, places, index_map)
+        name="front",
+    )(own, child, front, places, index_map)
 
 
 def from_behind(shard, by):
@@ -597,8 +600,7 @@
     own = front[:, :LEAD] + contribution(
         early_tiles, places[half : half + LEAD_BLOCKS], own_places
     )
-    rows, tiles = factor(own, child)
-    return exchange(rows, front, tiles, own_places[None], index_map.reshape(-1, BLOCK))[None]
+    return whole(own, child, front, own_places[None], index_map.reshape(-1, BLOCK))[None]
 
 
 def solution(mesh):

time: 171 us -> 159 us (0.930)
  the two profiles are of different devices: /device:TPU:12 before, /device:TPU:8 now
where the time goes in v4:
time: 159 us
  Pallas kernels  145 us (91%)
  local copies, waits for them, and re-layouts  5.13 us (3%)
  waiting for transfers between devices  3.55 us (2%)
  starting transfers between devices  2.38 us (1%)
  matrix products  1.87 us (1%)
    pallas_call x1, Pallas kernels, whole(): pl.pallas_call(front_kernel, out_shape=jax.ShapeDtypeStruct(front.shape,...  145 us
    unnamed x5, local copies, waits for them, and re-layouts  3.95 us
    ppermute x1, waiting for transfers between devices, from_behind(): lax.ppermute(shard, 'blk', [(i, (i + by) % count) for i in range(count)])  3.55 us
  transfers between devices with their start and end apart: 1, of which 1 were waited for; matrix products, arithmetic and copies ran while one was open for 1% of the time, Pallas kernels for 0%

profile of v4, /device:TPU:8, one launch (start us, length us, event | category | flops | bytes accessed | tf_op | source)
XLA Modules:
  0.0 159.2 jit_solution(7359033951352036254)
XLA Ops:
  0.0 0.9 slice.26
  0.9 2.4 %collective-permute-start = (f32[64,512]{1,0:T(8,128)S(1)}, f32[64,512]{1,0:T(8,128)S(1)}, u32[]{:S(2)}, u32[]{:S(2)}) collective-permute-start(f32[64,512]{1,0:T(8,128)S(1)} %slice.26), channel_id=1, source_target_pairs={{0,32},{1,33},{2,34},{3,35},{4,36},{5,37},{6,38},{7,39},{8,40},{9,... | collective-permute-start | bytes 393224 | tf_op jit(solution)/shard_map/ppermute | solution.py:577
  3.3 0.7 add_select_fusion
  4.0 0.1 reshape.25
  4.1 0.1 slice.22
  4.2 3.5 %collective-permute-done = f32[64,512]{1,0:T(8,128)S(1)} collective-permute-done((f32[64,512]{1,0:T(8,128)S(1)}, f32[64,512]{1,0:T(8,128)S(1)}, u32[]{:S(2)}, u32[]{:S(2)}) %collective-permute-start) | collective-permute-done | bytes 131104 | tf_op jit(solution)/shard_map/ppermute | solution.py:577
  7.7 0.1 reshape.26
  7.8 0.3 convolution_bitcast_fusion
  8.2 1.5 convolution_add_fusion.own_ref
  9.7 0.0 copy-start
  9.7 1.2 copy-done
  11.0 0.0 copy-start.1
  11.0 0.7 copy-done.1
  11.7 145.5 %front.1 = f32[128,8192]{1,0:T(8,128)S(1)} custom-call(f32[128,1024]{1,0:T(8,128)S(1)} %convolution_add_fusion.own_ref, f32[64,4096]{1,0:T(8,128)S(1)} %bitcast.14, f32[128,8192]{1,0:T(8,128)} %bitcast.17, s32[1,64]{1,0:T(1,128)S(1)} %constant_dynamic-slice_fusion.places_ref, s32[32,128]{1,0:T(8,128)S(1)} %bitcast.15), custom_call_target="tpu_custom_call" | custom-call | tf_op jit(solution)/shard_map/front/pallas_call | solution.py:533
  157.2 2.0 %copy.15 = f32[1,128,8192]{2,1,0:T(8,128)} copy(f32[1,128,8192]{2,1,0:T(8,128)S(1)} %bitcast.12) | data formatting | bytes 8388608
  (3 shorter events, 0.0 us)
Async XLA Ops:
  0.9 6.8 %collective-permute-start = (f32[64,512]{1,0:T(8,128)S(1)}, f32[64,512]{1,0:T(8,128)S(1)}, u32[]{:S(2)}, u32[]{:S(2)}) collective-permute-start(f32[64,512]{1,0:T(8,128)S(1)} %slice.26), channel_id=1, source_target_pairs={{0,32},{1,33},{2,34},{3,35},{4,36},{5,37},{6,38},{7,39},{8,40},{9,... | collective-permute-start | bytes 393224 | tf_op jit(solution)/shard_map/ppermute | solution.py:577
  9.7 1.2 copy-start
  11.0 0.7 copy-start.1

commit v5 on v4

--- a/solution.py
+++ b/solution.py
@@ -125,9 +125,9 @@
 def front_kernel(
     own_ref, child_ref, front_ref, places_ref, index_ref, out_ref,
     lead, work, a_ref, x_ref, inverses, tiles, staged,
-    line, plane, made, came, z_made, z_came, picked,
+    line, plane, made, came, z_made, z_came, two_made, two_came, picked,
     local_sem, b_send, a_send, b_recv, tile_sem, own_sem,
-    l_send, l_recv, p_send, p_recv, q_send, q_recv, z_send, z_recv,
+    l_send, l_recv, p_send, p_recv, q_send, q_recv, z_send, z_recv, two_send, two_recv,
 ):
     y, x, z = position()
     a = y * X + x
@@ -141,7 +141,8 @@
     def plane_device(slot):
         return {"blk": plane_index(slot) * Z + z}
 
-    greet([up, down] + [plane_device(slot) for slot in range(1, STEPS)])
+    up_two, down_two = device(y, x, z + 2), device(y, x, z - 2)
+    greet([up, down, up_two, down_two] + [plane_device(slot) for slot in range(1, STEPS)])
     base = pltpu.make_async_copy(front_ref, out_ref, local_sem.at[1])
     base.start()
     root = a == 0
@@ -394,8 +395,93 @@
     lax.fori_loop(0, LEAD_BLOCKS, step, 0)
     keep_rows(1)
     gather(1)
+    gather_first(1)
+    gather_second(1)
+    gather_third(1)
+    gather_last(0)
+    gather_last(1)
+
+    def lefts(block, holder, zz):
+        j = lax.broadcasted_iota(jnp.int32, (BLOCK, LEAD), 0) + lax.rem(zz + Z, Z) * BLOCK
+        q = lax.broadcasted_iota(jnp.int32, (BLOCK, LEAD), 1)
+        chosen = jnp.where(j == q, 1.0, 0.0).astype(jnp.bfloat16)
+        is_lead = jnp.full((BLOCK, LEAD), holder, jnp.int32) == 0
+        return jnp.where(is_lead, chosen, block)
+
+    def product(left_side, right_side):
+        return dot(left_side, right_side, ((1,), (1,)), None)
+
+    def first_of(slot):
+        return jnp.where(slot < X, 2, 3)
+
+    def product_copy(slot):
+        landing = slot // X * X + lax.rem(X - lax.rem(slot, X), X)
+        return remote(
+            made.at[slot], came.at[landing], q_send.at[slot], q_recv.at[landing], plane_device(slot)
+        )
+
+    def z_copy(way):
+        return remote(
+            z_made.at[way],
+            z_came.at[way],
+            z_send.at[way],
+            z_recv.at[way],
+            up if way == 0 else down,
+        )
+
+    two_slots = (range(1, X), range(X, STEPS))
+
+    def two_copy(way):
+        width = len(two_slots[way]) * BLOCK
+        return remote(
+            two_made.at[way, :, 0:width],
+            two_came.at[way, :, 0:width],
+            two_send.at[way],
+            two_recv.at[way],
+            up_two if way == 0 else down_two,
+        )
+
+    sends = a != 0
+
+    def slot_at(i):
+        return lax.rem(i * 5, STEPS)
+
+    def make(i, carry):
+        slot = slot_at(i)
+        block = plane[pl.ds(pl.multiple_of(slot * BLOCK, BLOCK), BLOCK)]
+        part = line[pl.ds(pl.multiple_of(first_of(slot) * BLOCK, BLOCK), 4 * BLOCK)]
+        made[slot] = product(lefts(block, plane_index(slot), z), part)
+
+        @pl.when(sends & (i > 1))
+        def _():
+            product_copy(slot_at(i - 1)).start()
+
+        return carry
+
+    lax.fori_loop(1, STEPS, make, 0)
+    two_made[0, :, 0 : (X - 1) * BLOCK] = product(
+        lefts(line[rows(2)], a, z + 2), plane[BLOCK : X * BLOCK]
+    )
+    pl.when(sends)(product_copy(slot_at(jnp.full((), STEPS - 1, jnp.int32))).start)
+    two_made[1] = product(lefts(line[rows(Z - 2)], a, z - 2), plane[X * BLOCK :])
+    two_copy(0).start()
+    z_made[0] = product(lefts(line[rows(1)], a, z + 1), plane[BLOCK:])
+    two_copy(1).start()
+    z_made[1] = product(lefts(line[rows(Z - 1)], a, z - 1), plane[BLOCK:])
+    z_copy(0).start()
+
+    def put(aa, zz, value):
+        block = aa * Z + lax.rem(zz + Z, Z)
+        columns = pl.ds(pl.multiple_of(block * BLOCK, BLOCK), BLOCK)
+        kept = jnp.where(jnp.full((BLOCK, BLOCK), aa, jnp.int32) == 0, 0.0, out_ref[:, columns] - value)
+        is_lead = jnp.full((BLOCK, BLOCK), a, jnp.int32) == 0
+        out_ref[:, columns] = jnp.where(is_lead, value, kept)
+
+    own = lefts(line[rows(0)], a, z)
+    along = product(own, line[...])
+    z_copy(1).start()
+    base.wait()
     tiles_copy.wait_recv()
-
     slot_of = lax.broadcasted_iota(jnp.int32, (BLOCK, TILE_WIDTH), 0)
     column_table = jnp.where(slot_of == places_ref[...], 1.0, 0.0).astype(jnp.float32)
     order = picked.shape[1]
@@ -412,71 +498,7 @@
         out_ref[:, columns] = out_ref[:, columns] + dot(part, row_table, ((1,), (1,)))
         return carry
 
-    gather_first(1)
-    base.wait()
-    lax.fori_loop(0, pairs // 4, place, 0)
-    gather_second(1)
-    lax.fori_loop(pairs // 4, pairs // 2, place, 0)
-    gather_third(1)
-    lax.fori_loop(pairs // 2, pairs, place, 0)
-    gather_last(0)
-    gather_last(1)
-
-    def lefts(block, holder, zz):
-        j = lax.broadcasted_iota(jnp.int32, (BLOCK, LEAD), 0) + lax.rem(zz + Z, Z) * BLOCK
-        q = lax.broadcasted_iota(jnp.int32, (BLOCK, LEAD), 1)
-        chosen = jnp.where(j == q, 1.0, 0.0).astype(jnp.bfloat16)
-        is_lead = jnp.full((BLOCK, LEAD), holder, jnp.int32) == 0
-        return jnp.where(is_lead, chosen, block)
-
-    def product(left_side, right_side):
-        return dot(left_side, right_side, ((1,), (1,)), None)
-
-    near = (2 * BLOCK, 7 * BLOCK)
-
-    def product_copy(slot):
-        landing = slot // X * X + lax.rem(X - lax.rem(slot, X), X)
-        return remote(
-            made.at[slot], came.at[landing], q_send.at[slot], q_recv.at[landing], plane_device(slot)
-        )
-
-    def z_copy(way):
-        return remote(
-            z_made.at[way],
-            z_came.at[way],
-            z_send.at[way],
-            z_recv.at[way],
-            up if way == 0 else down,
-        )
-
-    sends = a != 0
-
-    def make(slot, carry):
-        block = plane[pl.ds(pl.multiple_of(slot * BLOCK, BLOCK), BLOCK)]
-        made[slot] = product(lefts(block, plane_index(slot), z), line[near[0] : near[1]])
-
-        @pl.when(sends & (slot > 1))
-        def _():
-            product_copy(slot - 1).start()
-
-        return carry
-
-    lax.fori_loop(1, STEPS, make, 0)
-    z_made[0] = product(lefts(line[rows(1)], a, z + 1), plane[BLOCK:])
-    pl.when(sends)(product_copy(STEPS - 1).start)
-    z_made[1] = product(lefts(line[rows(Z - 1)], a, z - 1), plane[BLOCK:])
-    z_copy(0).start()
-
-    def put(aa, zz, value):
-        block = aa * Z + lax.rem(zz + Z, Z)
-        columns = pl.ds(pl.multiple_of(block * BLOCK, BLOCK), BLOCK)
-        kept = jnp.where(jnp.full((BLOCK, BLOCK), aa, jnp.int32) == 0, 0.0, out_ref[:, columns] - value)
-        is_lead = jnp.full((BLOCK, BLOCK), a, jnp.int32) == 0
-        out_ref[:, columns] = jnp.where(is_lead, value, kept)
-
-    own = lefts(line[rows(0)], a, z)
-    along = product(own, line[...])
-    z_copy(1).start()
+    lax.fori_loop(0, pairs, place, 0)
     for s in range(Z):
         put(a, z + s, along[:, s * BLOCK : (s + 1) * BLOCK])
     along = product(own, plane[BLOCK:])
@@ -487,21 +509,29 @@
         for slot in range(1, STEPS):
             value = z_came[way, :, (slot - 1) * BLOCK : slot * BLOCK]
             put(plane_index(slot), z - 1 if way == 0 else z + 1, value)
-
-    def take(slot, carry):
+    for way in (0, 1):
+        two_copy(way).wait_recv()
+        for i, slot in enumerate(two_slots[way]):
+            value = two_came[way, :, i * BLOCK : (i + 1) * BLOCK]
+            put(plane_index(slot), z - 2 if way == 0 else z + 2, value)
+
+    def take(i, carry):
+        slot = slot_at(i)
         source = plane_index(slot)
 
         @pl.when(source != 0)
         def _():
             landing = slot // X * X + lax.rem(X - lax.rem(slot, X), X)
             product_copy(landing).wait_recv()
-            for s in range(2, Z - 1):
-                put(source, z + s, came[slot, :, (s - 2) * BLOCK : (s - 1) * BLOCK])
+            for s in range(4):
+                value = came[slot, :, s * BLOCK : (s + 1) * BLOCK]
+                put(source, z + first_of(slot) + s, value)
 
         @pl.when(source == 0)
         def _():
-            for s in range(2, Z - 1):
-                columns = pl.ds(pl.multiple_of(lax.rem(z + s, Z) * BLOCK, BLOCK), BLOCK)
+            for s in range(4):
+                zz = lax.rem(z + first_of(slot) + s, Z)
+                columns = pl.ds(pl.multiple_of(zz * BLOCK, BLOCK), BLOCK)
                 out_ref[:, columns] = jnp.zeros((BLOCK, BLOCK), jnp.float32)
 
         return carry
@@ -511,6 +541,7 @@
         pl.when(sends)(product_copy(slot).wait_send)
     for way in (0, 1):
         z_copy(way).wait_send()
+        two_copy(way).wait_send()
     tiles_copy.wait_send()
     for panel in (0, 1):
         for way in (0, 1):
@@ -545,10 +576,12 @@
             pltpu.VMEM((2, BLOCK, PANEL_WIDTH), bf16),
             pltpu.VMEM((Z * BLOCK, LEAD), bf16),
             pltpu.VMEM((STEPS * BLOCK, LEAD), bf16),
-            pltpu.VMEM((STEPS, BLOCK, 5 * BLOCK), f32),
-            pltpu.VMEM((STEPS, BLOCK, 5 * BLOCK), f32),
+            pltpu.VMEM((STEPS, BLOCK, 4 * BLOCK), f32),
+            pltpu.VMEM((STEPS, BLOCK, 4 * BLOCK), f32),
             pltpu.VMEM((2, BLOCK, 7 * BLOCK), f32),
             pltpu.VMEM((2, BLOCK, 7 * BLOCK), f32),
+            pltpu.VMEM((2, BLOCK, 4 * BLOCK), f32),
+            pltpu.VMEM((2, BLOCK, 4 * BLOCK), f32),
             pltpu.VMEM((BLOCK, child.shape[1]), f32),
             dma((2,)),
             dma((LEAD_BLOCKS, LEAD // PIECE, 2)),
@@ -564,6 +597,8 @@
             dma((STEPS,)),
             dma((2,)),
             dma((2,)),
+            dma((2,)),
+            dma((2,)),
         ],
         compiler_params=pltpu.CompilerParams(
             collective_id=0, has_side_effects=True, vmem_limit_bytes=48 * MIB

time: 159 us -> 154 us (0.969); the launches traced: 159 us -> 152 us
  Pallas kernels: 145 us -> 138 us
    pallas_call x1, Pallas kernels: 145 us -> 138 us  [whole(): pl.pallas_call(front_kernel, out_shape=jax.ShapeDtypeStruct(front.shape,...]
where the time goes in v5:
time: 154 us; the launch traced here: 152 us
  Pallas kernels  138 us (90%)
  local copies, waits for them, and re-layouts  5.13 us (3%)
  waiting for transfers between devices  3.55 us (2%)
  starting transfers between devices  2.38 us (2%)
  matrix products  1.87 us (1%)
    pallas_call x1, Pallas kernels, whole(): pl.pallas_call(front_kernel, out_shape=jax.ShapeDtypeStruct(front.shape,...  138 us
    unnamed x5, local copies, waits for them, and re-layouts  3.95 us
    ppermute x1, waiting for transfers between devices, from_behind(): lax.ppermute(shard, 'blk', [(i, (i + by) % count) for i in range(count)])  3.55 us
  transfers between devices with their start and end apart: 1, of which 1 were waited for; matrix products, arithmetic and copies ran while one was open for 1% of the time, Pallas kernels for 0%

profile of v5, /device:TPU:8, one launch (start us, length us, event | category | flops | bytes accessed | tf_op | source)
XLA Modules:
  0.0 152.0 jit_solution(4150655529611689363)
XLA Ops:
  0.0 0.9 slice.26
  0.9 2.4 %collective-permute-start = (f32[64,512]{1,0:T(8,128)S(1)}, f32[64,512]{1,0:T(8,128)S(1)}, u32[]{:S(2)}, u32[]{:S(2)}) collective-permute-start(f32[64,512]{1,0:T(8,128)S(1)} %slice.26), channel_id=1, source_target_pairs={{0,32},{1,33},{2,34},{3,35},{4,36},{5,37},{6,38},{7,39},{8,40},{9,... | collective-permute-start | bytes 393224 | tf_op jit(solution)/shard_map/ppermute | solution.py:612
  3.3 0.7 add_select_fusion
  4.0 0.1 reshape.25
  4.1 0.1 slice.22
  4.2 3.5 %collective-permute-done = f32[64,512]{1,0:T(8,128)S(1)} collective-permute-done((f32[64,512]{1,0:T(8,128)S(1)}, f32[64,512]{1,0:T(8,128)S(1)}, u32[]{:S(2)}, u32[]{:S(2)}) %collective-permute-start) | collective-permute-done | bytes 131104 | tf_op jit(solution)/shard_map/ppermute | solution.py:612
  7.7 0.1 reshape.26
  7.8 0.3 convolution_bitcast_fusion
  8.2 1.5 %convolution_add_fusion.own_ref = f32[128,1024]{1,0:T(8,128)S(1)} fusion(f32[128,8192]{1,0:T(8,128)} %bitcast.16, f32[8,8,8,128]{3,2,1,0:T(8,128)S(1)} %convolution_bitcast_fusion, s32[64]{0:T(128)S(1)} %fusion.6), kind=kOutput, calls=%fused_computation | convolution fusion | flops 100802560 | bytes 1310976 | tf_op jit(solution)/shard_map/cq,cn->qn/dot_general | solution.py:621
  9.7 0.0 copy-start
  9.7 1.2 copy-done
  11.0 0.0 copy-start.1
  11.0 0.7 copy-done.1
  11.7 138.3 %front.1 = f32[128,8192]{1,0:T(8,128)S(1)} custom-call(f32[128,1024]{1,0:T(8,128)S(1)} %convolution_add_fusion.own_ref, f32[64,4096]{1,0:T(8,128)S(1)} %bitcast.14, f32[128,8192]{1,0:T(8,128)} %bitcast.17, s32[1,64]{1,0:T(1,128)S(1)} %constant_dynamic-slice_fusion.places_ref, s32[32,128]{1,0:T(8,128)S(1)} %bitcast.15), custom_call_target="tpu_custom_call" | custom-call | tf_op jit(solution)/shard_map/front/pallas_call | solution.py:564
  149.9 2.0 %copy.15 = f32[1,128,8192]{2,1,0:T(8,128)} copy(f32[1,128,8192]{2,1,0:T(8,128)S(1)} %bitcast.12) | data formatting | bytes 8388608
  (3 shorter events, 0.0 us)
Async XLA Ops:
  0.9 6.8 %collective-permute-start = (f32[64,512]{1,0:T(8,128)S(1)}, f32[64,512]{1,0:T(8,128)S(1)}, u32[]{:S(2)}, u32[]{:S(2)}) collective-permute-start(f32[64,512]{1,0:T(8,128)S(1)} %slice.26), channel_id=1, source_target_pairs={{0,32},{1,33},{2,34},{3,35},{4,36},{5,37},{6,38},{7,39},{8,40},{9,... | collective-permute-start | bytes 393224 | tf_op jit(solution)/shard_map/ppermute | solution.py:612
  9.7 1.2 copy-start
  11.0 0.7 copy-start.1

commit v6 on v5

--- a/solution.py
+++ b/solution.py
@@ -152,13 +152,18 @@
             return pl.ds(slot * BLOCK, BLOCK)
         return pl.ds(slot * BLOCK + half * (BLOCK // 2), BLOCK // 2)
 
-    def panel_columns(panel):
-        return pl.ds(panel * PANEL_WIDTH, PANEL_WIDTH)
+    parts_of = ((0,), (1, 2))
+
+    def part_columns(part):
+        narrow = PANEL_WIDTH // 2
+        return pl.ds(0, PANEL_WIDTH) if part == 0 else pl.ds((part + 1) * narrow, narrow)
 
     def own_copies(panel):
         return [
             pltpu.make_async_copy(
-                staged.at[panel], target.at[rows(0), panel_columns(panel)], own_sem.at[panel, i]
+                staged.at[panel],
+                target.at[rows(0), pl.ds(panel * PANEL_WIDTH, PANEL_WIDTH)],
+                own_sem.at[panel, i],
             )
             for i, target in enumerate((line, plane))
         ]
@@ -173,19 +178,19 @@
         for copy in own_copies(panel):
             copy.start()
 
-    def line_copy(panel, way, hop):
+    def line_copy(part, way, hop):
         half = None if hop < Z // 2 else way
         sign = -1 if way == 0 else 1
         start, end = (sign * (hop - 1)) % Z, (sign * hop) % Z
         return remote(
-            line.at[rows(start, half), panel_columns(panel)],
-            line.at[rows(end, half), panel_columns(panel)],
-            l_send.at[panel, way, hop - 1],
-            l_recv.at[panel, way, hop - 1],
+            line.at[rows(start, half), part_columns(part)],
+            line.at[rows(end, half), part_columns(part)],
+            l_send.at[part, way, hop - 1],
+            l_recv.at[part, way, hop - 1],
             up if way == 0 else down,
         )
 
-    def across(panel, number):
+    def across(part, number):
         start, end, half, target = [
             (0, 4, None, over),
             (0, 3, None, right),
@@ -198,51 +203,53 @@
             (5, 6, 1, left),
         ][number]
         return remote(
-            plane.at[rows(start, half), panel_columns(panel)],
-            plane.at[rows(end, half), panel_columns(panel)],
-            p_send.at[panel, number],
-            p_recv.at[panel, number],
+            plane.at[rows(start, half), part_columns(part)],
+            plane.at[rows(end, half), part_columns(part)],
+            p_send.at[part, number],
+            p_recv.at[part, number],
             target,
         )
 
     def gather(panel):
         along, beside = own_copies(panel)
         along.wait()
-        line_copy(panel, 0, 1).start()
-        line_copy(panel, 1, 1).start()
+        for part in parts_of[panel]:
+            line_copy(part, 0, 1).start()
+            line_copy(part, 1, 1).start()
         beside.wait()
-        for number in (0, 1, 2):
-            across(panel, number).start()
-
-    def pass_on(panel, hop):
+        for part in parts_of[panel]:
+            for number in (0, 1, 2):
+                across(part, number).start()
+
+    def pass_on(part, hop):
         for way in (0, 1):
-            line_copy(panel, way, hop).wait_recv()
-            line_copy(panel, way, hop + 1).start()
-
-    def pass_across(panel, number, *onward):
-        across(panel, number).wait_recv()
+            line_copy(part, way, hop).wait_recv()
+            line_copy(part, way, hop + 1).start()
+
+    def pass_across(part, number, *onward):
+        across(part, number).wait_recv()
         for other in onward:
-            across(panel, other).start()
-
-    def gather_first(panel):
-        pass_on(panel, 1)
-        pass_across(panel, 0, 3, 4)
-        pass_across(panel, 1, 5)
-        pass_across(panel, 2, 6)
-
-    def gather_second(panel):
-        pass_on(panel, 2)
-        pass_across(panel, 3, 7)
-        pass_across(panel, 4, 8)
-
-    def gather_third(panel):
-        pass_on(panel, 3)
-
-    def gather_last(panel):
+            across(part, other).start()
+
+    def gather_first(part):
+        pass_on(part, 1)
+        pass_across(part, 0, 3, 4)
+        pass_across(part, 1, 5)
+        pass_across(part, 2, 6)
+
+    def gather_second(part):
+        pass_on(part, 2)
+        pass_across(part, 3, 7)
+        pass_across(part, 4, 8)
+
+    def gather_third(part):
+        pass_on(part, 3)
+
+    def gather_last(part):
         for number in (5, 6, 7, 8):
-            across(panel, number).wait_recv()
+            across(part, number).wait_recv()
         for way in (0, 1):
-            line_copy(panel, way, Z // 2).wait_recv()
+            line_copy(part, way, Z // 2).wait_recv()
 
     def piece(s, span, send, target):
         p, c0, c1 = span
@@ -395,11 +402,11 @@
     lax.fori_loop(0, LEAD_BLOCKS, step, 0)
     keep_rows(1)
     gather(1)
-    gather_first(1)
-    gather_second(1)
-    gather_third(1)
-    gather_last(0)
-    gather_last(1)
+    for act in (gather_first, gather_second, gather_third):
+        for part in parts_of[1]:
+            act(part)
+    for part in (0, 1, 2):
+        gather_last(part)
 
     def lefts(block, holder, zz):
         j = lax.broadcasted_iota(jnp.int32, (BLOCK, LEAD), 0) + lax.rem(zz + Z, Z) * BLOCK
@@ -543,12 +550,12 @@
         z_copy(way).wait_send()
         two_copy(way).wait_send()
     tiles_copy.wait_send()
-    for panel in (0, 1):
+    for part in (0, 1, 2):
         for way in (0, 1):
             for hop_number in range(1, Z // 2 + 1):
-                line_copy(panel, way, hop_number).wait_send()
+                line_copy(part, way, hop_number).wait_send()
         for number in range(9):
-            across(panel, number).wait_send()
+            across(part, number).wait_send()
     for s in range(LEAD_BLOCKS):
         away = lax.rem(z - s + Z, Z)
         for span in pieces_of(s, True) + pieces_of(s, False):
@@ -589,10 +596,10 @@
             dma((LEAD_BLOCKS, LEAD // PIECE)),
             dma((2,)),
             dma((2, 2)),
-            dma((2, 2, Z // 2)),
-            dma((2, 2, Z // 2)),
-            dma((2, 9)),
-            dma((2, 9)),
+            dma((3, 2, Z // 2)),
+            dma((3, 2, Z // 2)),
+            dma((3, 9)),
+            dma((3, 9)),
             dma((STEPS,)),
             dma((STEPS,)),
             dma((2,)),

time: 154 us -> 155 us (level)
  Pallas kernels: 138 us -> 140 us
    pallas_call x1, Pallas kernels: 138 us -> 140 us  [whole(): pl.pallas_call(front_kernel, out_shape=jax.ShapeDtypeStruct(front.shape,...]
where the time goes in v6:
time: 155 us; the launch traced here: 154 us
  Pallas kernels  140 us (90%)
  local copies, waits for them, and re-layouts  5.13 us (3%)
  waiting for transfers between devices  3.55 us (2%)
  starting transfers between devices  2.38 us (2%)
  matrix products  1.87 us (1%)
    pallas_call x1, Pallas kernels, whole(): pl.pallas_call(front_kernel, out_shape=jax.ShapeDtypeStruct(front.shape,...  140 us
    unnamed x5, local copies, waits for them, and re-layouts  3.95 us
    ppermute x1, waiting for transfers between devices, from_behind(): lax.ppermute(shard, 'blk', [(i, (i + by) % count) for i in range(count)])  3.55 us
  transfers between devices with their start and end apart: 1, of which 1 were waited for; matrix products, arithmetic and copies ran while one was open for 1% of the time, Pallas kernels for 0%

profile of v6, /device:TPU:8, one launch (start us, length us, event | category | flops | bytes accessed | tf_op | source)
XLA Modules:
  0.0 154.0 jit_solution(13565844720440852496)
XLA Ops:
  0.0 0.9 slice.26
  0.9 2.4 %collective-permute-start = (f32[64,512]{1,0:T(8,128)S(1)}, f32[64,512]{1,0:T(8,128)S(1)}, u32[]{:S(2)}, u32[]{:S(2)}) collective-permute-start(f32[64,512]{1,0:T(8,128)S(1)} %slice.26), channel_id=1, source_target_pairs={{0,32},{1,33},{2,34},{3,35},{4,36},{5,37},{6,38},{7,39},{8,40},{9,... | collective-permute-start | bytes 393224 | tf_op jit(solution)/shard_map/ppermute | solution.py:619
  3.3 0.7 add_select_fusion
  4.0 0.1 reshape.25
  4.1 0.1 slice.22
  4.2 3.5 %collective-permute-done = f32[64,512]{1,0:T(8,128)S(1)} collective-permute-done((f32[64,512]{1,0:T(8,128)S(1)}, f32[64,512]{1,0:T(8,128)S(1)}, u32[]{:S(2)}, u32[]{:S(2)}) %collective-permute-start) | collective-permute-done | bytes 131104 | tf_op jit(solution)/shard_map/ppermute | solution.py:619
  7.7 0.1 reshape.26
  7.8 0.3 convolution_bitcast_fusion
  8.2 1.5 convolution_add_fusion.own_ref
  9.7 0.0 copy-start
  9.7 1.2 copy-done
  11.0 0.0 copy-start.1
  11.0 0.7 copy-done.1
  11.7 140.3 %front.1 = f32[128,8192]{1,0:T(8,128)S(1)} custom-call(f32[128,1024]{1,0:T(8,128)S(1)} %convolution_add_fusion.own_ref, f32[64,4096]{1,0:T(8,128)S(1)} %bitcast.14, f32[128,8192]{1,0:T(8,128)} %bitcast.17, s32[1,64]{1,0:T(1,128)S(1)} %constant_dynamic-slice_fusion.places_ref, s32[32,128]{1,0:T(8,128)S(1)} %bitcast.15), custom_call_target="tpu_custom_call" | custom-call | tf_op jit(solution)/shard_map/front/pallas_call | solution.py:571
  152.0 2.0 %copy.15 = f32[1,128,8192]{2,1,0:T(8,128)} copy(f32[1,128,8192]{2,1,0:T(8,128)S(1)} %bitcast.12) | data formatting | bytes 8388608
  (3 shorter events, 0.0 us)
Async XLA Ops:
  0.9 6.8 %collective-permute-start = (f32[64,512]{1,0:T(8,128)S(1)}, f32[64,512]{1,0:T(8,128)S(1)}, u32[]{:S(2)}, u32[]{:S(2)}) collective-permute-start(f32[64,512]{1,0:T(8,128)S(1)} %slice.26), channel_id=1, source_target_pairs={{0,32},{1,33},{2,34},{3,35},{4,36},{5,37},{6,38},{7,39},{8,40},{9,... | collective-permute-start | bytes 393224 | tf_op jit(solution)/shard_map/ppermute | solution.py:619
  9.7 1.2 copy-start
  11.0 0.7 copy-start.1
